TPU v7x, 1024 devices: a whole 4x4x32 slice. The times are simulated.
1024 devices in a mesh: expert: 16 (over y, x), fsdp: 64 (over z, core).
Axes of the slice: x: 4, y: 4, z: 32, core: 2. Of those that a mesh axis runs over, the one named last changes fastest.
Arguments:
- out_grad: bfloat16 [262144, 2048], P(('expert', 'fsdp')), may hold values from -0.059814453 to 0.059814453
- expert_ids: int32 [262144, 1], P(('expert', 'fsdp')), may hold values from 0 to 15; in each aligned block of 256 rows (0 to 255, 256 to 511, ...) at most 24 rows name the same one
- route_gates: float32 [262144, 1], P(('expert', 'fsdp')), may hold values from 0.2 to 1
- hidden_saved: bfloat16 [16, 64, 16, 24, 768], P('expert', 'fsdp'), may hold values from -6 to 6
- momentum: float32 [16, 2048, 768], P('expert', 'fsdp'), may hold values from -30 to 30
Outputs:
- new_momentum: float32 [16, 2048, 768], P('expert', 'fsdp')
- update: float32 [16, 2048, 768], P('expert', 'fsdp')
Inputs may be any that keep to these rules, and one draw needn't show every extreme that they name: `expert_ids`: in each aligned block of 256 tokens (the tokens of one device) no expert is named by more than 24 routes, and in some block one expert is named by exactly 24.
All inputs are finite; a program needn't handle non-finite values.
Results may differ from a plain program's by a relative error of at most 0.0028.
Values may be sent and summed in bfloat16 or wider, within the bound.
No kernel may reach another device: no remote copies, remote signals or barrier semaphores. Data moves between devices by JAX's collectives and lax.ppermute only.
A program may use at most 32 MiB of HBM per device.

v0:
```python
import math

import jax
import jax.numpy as jnp
from jax import lax
from jax.sharding import Mesh
from jax.sharding import PartitionSpec as P

D = 2048
FSDP = ("fsdp_0", "fsdp_1")
EXPERT_FSDP = ("expert", "fsdp_0", "fsdp_1")


QUINTIC = (3.4445, -4.775, 2.0315)
DECAY = 0.95
EPSILON = 1e-07


def reduced_to_own(pieces, axes, turns):
    inside = pieces.shape[1:]
    pieces = pieces.reshape(*(lax.axis_size(a) for a in axes), *inside)
    pieces = jnp.moveaxis(pieces, turns, range(len(axes))).reshape(-1, *inside)
    for k in turns:
        pieces = lax.psum_scatter(pieces, axes[k], scatter_dimension=0, tiled=True)
    return pieces[0]


def cut_along(x, dim, peers):
    dims = x.shape
    pieces = x.reshape(*dims[:dim], peers, dims[dim] // peers, *dims[dim + 1 :])
    return jnp.moveaxis(pieces, dim, 0)


def scatter_axes(x, axes, turns, dim):
    peers = lax.axis_size(axes)
    return reduced_to_own(cut_along(x, dim, peers), axes, turns)


def slab_times(matrix, gram):
    return jnp.einsum("edf,efg->edg", matrix, gram, precision=lax.Precision.HIGHEST)


def local(out_grad, expert_ids, route_gates, hidden_saved, momentum):
    n_expert = lax.axis_size("expert")
    exp_dev, d_local, hidden_units = momentum.shape
    tok_rows, features = out_grad.shape
    routes = expert_ids.shape[1]
    capacity = hidden_saved.shape[3]
    experts = exp_dev * n_expert
    routed = (route_gates[:, :, None] * out_grad[:, None, :].astype(jnp.float32)).astype(
        jnp.bfloat16
    )
    routed = routed.reshape(tok_rows * routes, features)
    flat_ids = expert_ids.reshape(-1)
    one_hot = (flat_ids[:, None] == jnp.arange(experts, dtype=jnp.int32)[None, :]).astype(jnp.int32)
    order_rank = jnp.cumsum(one_hot, axis=0) - one_hot
    slot_index = jnp.sum(order_rank * one_hot, axis=1)
    target = flat_ids * capacity + slot_index
    placing = (target[:, None] == jnp.arange(experts * capacity, dtype=jnp.int32)[None, :]).astype(
        jnp.bfloat16
    )
    outgoing = jnp.dot(placing.T, routed, preferred_element_type=jnp.float32).astype(jnp.bfloat16)
    outgoing = outgoing.reshape(n_expert, exp_dev, capacity, features)
    received = lax.all_to_all(outgoing, "expert", split_axis=0, concat_axis=0, tiled=True)
    gathered = jnp.transpose(received, (1, 0, 2, 3)).reshape(exp_dev, n_expert * capacity, features)
    saved_rows = hidden_saved.reshape(exp_dev, n_expert * capacity, hidden_units)
    full_term = jnp.einsum("erd,erf->def", gathered, saved_rows, preferred_element_type=jnp.float32)
    full_term = full_term.reshape(features, exp_dev * hidden_units)
    summed = scatter_axes(full_term, FSDP, (1, 0), 0)
    gradient = jnp.transpose(summed.reshape(d_local, exp_dev, hidden_units), (1, 0, 2))
    moment_new = DECAY * momentum + gradient
    velocity = gradient + DECAY * moment_new
    gram_part = jnp.einsum("edf,edg->efg", velocity, velocity, precision=lax.Precision.HIGHEST)
    tile_size = math.gcd(hidden_units, 128)
    tile_count = hidden_units // tile_size
    tile_pairs = [(i, j) for i in range(tile_count) for j in range(i, tile_count)]
    lookup = {}
    for number, pair_item in enumerate(tile_pairs):
        lookup[pair_item] = number
    packed = jnp.stack(
        [
            gram_part[:, i * tile_size : (i + 1) * tile_size, j * tile_size : (j + 1) * tile_size]
            for i, j in tile_pairs
        ],
        axis=1,
    )
    summed_tiles = lax.psum(packed, FSDP)
    tile_rows = []
    for i in range(tile_count):
        pieces = []
        for j in range(tile_count):
            if i <= j:
                pieces.append(summed_tiles[:, lookup[i, j]])
            else:
                pieces.append(jnp.swapaxes(summed_tiles[:, lookup[j, i]], 1, 2))
        tile_rows.append(jnp.concatenate(pieces, axis=2))
    gram_full = jnp.concatenate(tile_rows, axis=1)
    square_sum = jnp.trace(gram_full, axis1=1, axis2=2) + EPSILON
    start_x = velocity / jnp.sqrt(square_sum)[:, None, None]
    gram_zero = gram_full / square_sum[:, None, None]

    def apply_first(matrix):
        once = slab_times(matrix, gram_zero)
        return QUINTIC[0] * matrix + QUINTIC[1] * once + QUINTIC[2] * slab_times(once, gram_zero)

    def apply_second(matrix):
        return apply_first(slab_times(apply_first(matrix), gram_zero))

    next_x = apply_first(start_x)
    once_more = apply_second(next_x)
    twice_more = apply_second(once_more)
    final_x = QUINTIC[0] * next_x + QUINTIC[1] * once_more + QUINTIC[2] * twice_more
    return (moment_new, final_x * jnp.sqrt(jnp.float32(D)))


def solution(mesh):
    finer = Mesh(mesh.devices.reshape(mesh.shape["expert"], 32, 2), ("expert", "fsdp_0", "fsdp_1"))
    placed = (
        P(EXPERT_FSDP, None),
        P(EXPERT_FSDP, None),
        P(EXPERT_FSDP, None),
        P("expert", FSDP, None, None, None),
        P("expert", FSDP, None),
    )
    return jax.shard_map(
        local,
        mesh=finer,
        in_specs=placed,
        out_specs=(P("expert", FSDP, None), P("expert", FSDP, None)),
        check_vma=False,
    )
```

profile of v0, /device:TPU:1, one launch (start us, length us, event | category | flops | bytes accessed | tf_op | source)
XLA Modules:
  0.0 688.9 jit_solution(17033827825847857764)
XLA Ops:
  7.2 0.7 fusion.22
  8.8 0.8 fusion.21
  10.2 1.9 convolution_convert_fusion
  12.2 22.2 %all_to_all.5 = bf16[16,1,24,2048]{3,2,1,0:T(8,128)(2,1)S(1)} all-to-all(bf16[16,1,24,2048]{3,2,1,0:T(8,128)(2,1)S(1)} %bitcast.296), channel_id=1, replica_groups=mesh['expert'=16,'fsdp_0'=32,'fsdp_1'=2] {'expert'}, dimensions={0} | all-to-all | bytes 3145728 | tf_op jit(solution)/shard_map/all_to_all | solution.py:64
  34.4 1.9 fusion.23
  36.3 3.4 copy.46
  39.7 48.6 %reduce-scatter.3.cloned.1.call-done = f32[32,32,768]{2,1,0:T(8,128)} async-done(((f32[64,32,768]{2,1,0:T(8,128)}), f32[32,32,768]{2,1,0:T(8,128)}) %reduce-scatter.3.cloned.1.call-update) | async-done | bytes 3145744 | tf_op jit(solution)/shard_map/reduce_scatter | solution.py:24
  88.6 123.4 %reduce-scatter.5.cloned.1.call-done = f32[1,32,768]{2,1,0:T(8,128)} async-done(((f32[32,32,768]{2,1,0:T(8,128)}), f32[1,32,768]{2,1,0:T(8,128)}) %reduce-scatter.5.cloned.1.call-update) | async-done | bytes 98320 | tf_op jit(solution)/shard_map/reduce_scatter | solution.py:24
  212.0 0.9 multiply_add_fusion.1
  212.9 3.1 convolution_bitcast_fusion
  216.3 1.1 copy-done.5
  217.4 425.8 %all-reduce.2.cloned.1.call-done = f32[1,21,128,128]{3,2,1,0:T(8,128)} async-done(((f32[1,21,128,128]{3,2,1,0:T(8,128)}), f32[1,21,128,128]{3,2,1,0:T(8,128)}) %all-reduce.2.cloned.1.call-update) | async-done | bytes 1376272 | tf_op jit(solution)/shard_map/psum | solution.py:87
  643.2 1.4 slice_bitcast_fusion.25
  648.2 0.7 copy-done.8
  649.0 1.2 copy.62
  651.4 1.9 copy.63
  657.3 0.7 copy-done.6
  658.1 1.6 constant_dynamic-update-slice_fusion.45
  659.7 1.0 bitcast_dynamic-update-slice_fusion.2
  660.8 1.0 bitcast_dynamic-update-slice_fusion.1
  664.1 1.4 fusion.16
  665.6 1.4 fusion.2
  667.0 1.4 fusion.14
  668.5 1.4 fusion.4
  669.9 1.4 fusion.24
  671.4 1.4 fusion.25
  672.8 1.7 fusion.5
  674.5 1.4 fusion.26
  675.9 1.4 fusion.6
  677.4 1.4 fusion.27
  678.8 1.4 fusion.28
  680.3 2.1 fusion.11
  (97 shorter events, 12.4 us)
Async XLA Ops:
  7.2 27.3 %copy-start = (bf16[1,1,16,24,768]{4,3,2,1,0:T(8,128)(2,1)S(1)}, bf16[1,1,16,24,768]{4,3,2,1,0:T(8,128)(2,1)}, u32[]{:S(2)}) copy-start(bf16[1,1,16,24,768]{4,3,2,1,0:T(8,128)(2,1)} %param.8) | copy-start | bytes 1769476
  7.2 81.1 %reduce-scatter.3.cloned.1.call-start = ((), (), s32[]{:S(2)}) async-start(), calls=%async_computation.3 | async-start | bytes 9437184 | tf_op jit(solution)/shard_map/reduce_scatter | solution.py:24
  39.7 172.3 %copy-start.10 = (f32[1,32,768]{2,1,0:T(8,128)S(1)}, f32[1,32,768]{2,1,0:T(8,128)}, u32[]{:S(2)}) copy-start(f32[1,32,768]{2,1,0:T(8,128)} %param.9) | copy-start | bytes 294916
  39.7 172.3 %reduce-scatter.5.cloned.1.call-start = ((), (), s32[]{:S(2)}) async-start(), calls=%async_computation.4 | async-start | bytes 3244032 | tf_op jit(solution)/shard_map/reduce_scatter | solution.py:24
  88.3 554.8 %all-reduce.2.cloned.1.call-start = ((), (), s32[]{:S(2)}) async-start(), calls=%async_computation.5 | async-start | bytes 2752512 | tf_op jit(solution)/shard_map/psum | solution.py:87
  212.9 452.7 %copy-start.2 = (f32[1,32,768]{2,1,0:T(8,128)}, f32[1,32,768]{2,1,0:T(8,128)S(1)}, u32[]{:S(2)}) copy-start(f32[1,32,768]{2,1,0:T(8,128)S(1)} %multiply_add_fusion.1) | copy-start | bytes 294916
  216.3 1.1 copy-start.5
  643.2 4.2 copy-start.1
  647.4 0.8 copy-start.9
  648.2 0.7 copy-start.8
  653.3 7.4 %copy-start.4 = (f32[128,768]{1,0:T(8,128)S(1)}, f32[128,768]{1,0:T(8,128)}, u32[]{:S(2)}) copy-start(f32[128,768]{1,0:T(8,128)} %copy.63) | copy-start | bytes 1179652
  657.3 0.8 copy-start.6
  658.0 3.8 copy-start.7
  663.2 0.9 copy-start.3
Sparse Core Ops, SparseCore 0:
  39.8 48.4 reduce-scatter.2
  91.7 120.1 reduce-scatter.4
  217.5 425.5 all-reduce.1
where the time goes:
time: 689 us
  waiting for transfers between devices  598 us (87%)
  matrix products  25 us (4%)
  local copies, waits for them, and re-layouts  23.9 us (3%)
  blocking collectives  22.2 us (3%)
  between operations  15.1 us (2%)
    psum x1, waiting for transfers between devices, local(): summed_tiles = lax.psum(packed, FSDP)  426 us
    reduce_scatter x2, waiting for transfers between devices, reduced_to_own(): pieces = lax.psum_scatter(pieces, axes[k], scatter_dimension=0, tiled=True)  172 us
    all_to_all x1, blocking collectives, local(): lax.all_to_all(outgoing, 'expert', split_axis=0, concat_axis=0, tiled=True)  22.2 us
    dot_general x12, matrix products, slab_times(): jnp.einsum('edf,efg->edg', matrix, gram, precision=lax.Precision.HIGHEST)  18.2 us
  transfers between devices with their start and end apart: 3, of which 3 were waited for; matrix products, arithmetic and copies ran while one was open for 0% of the time, Pallas kernels for 0%

commit v1 on v0

v1 whole, which is shorter than its diff:
```python
import jax
import jax.numpy as jnp
from jax import lax
from jax.experimental import pallas as pl
from jax.experimental.pallas import tpu as pltpu
from jax.sharding import Mesh
from jax.sharding import PartitionSpec as P

D = 2048
FSDP = ("z", "core")
EXPERT_FSDP = ("expert", "z", "core")

QUINTIC = (3.4445, -4.775, 2.0315)
DECAY = 0.95
EPSILON = 1e-07

STRIDE = 3
REACH = 5
FAR = range(-REACH, REACH + 1)
UP = tuple(a for a in FAR if a < REACH)
DOWN = tuple(FAR)
OFFSETS = (
    tuple(STRIDE * a + 1 for a in UP)
    + tuple(STRIDE * a - 1 for a in DOWN)
    + tuple(STRIDE * a for a in FAR)
)
NARROW = (5, 4)


def shifted(x, by, ring):
    return lax.ppermute(x, "z", [(i, (i + by) % ring) for i in range(ring)])


def swapped(x):
    return lax.ppermute(x, "core", [(0, 1), (1, 0)])


def route_kernel(ids_ref, gates_ref, grad_ref, out_ref, *, experts, capacity):
    rows, features = grad_ref.shape
    slots = experts * capacity
    f32, bf16 = jnp.float32, jnp.bfloat16
    ids = ids_ref[...]
    one_hot = lax.broadcasted_iota(jnp.int32, (experts, rows), 0) == ids
    one_hot = jnp.where(one_hot, 1.0, 0.0).astype(f32)
    r = lax.broadcasted_iota(jnp.int32, (rows, rows), 0)
    c = lax.broadcasted_iota(jnp.int32, (rows, rows), 1)
    earlier = jnp.where(r < c, 1.0, 0.0).astype(bf16)
    rank = jnp.dot(one_hot.astype(bf16), earlier, preferred_element_type=f32)
    slot = jnp.sum(rank * one_hot, axis=0, keepdims=True)
    target = ids.astype(f32) * float(capacity) + slot
    place = lax.broadcasted_iota(jnp.int32, (slots, rows), 0).astype(f32)
    placing = jnp.where(place == target, 1.0, 0.0).astype(bf16)
    gates = jnp.transpose(jnp.broadcast_to(gates_ref[...], (128, rows)))[:, 0:1]
    routed = (gates * grad_ref[...].astype(f32)).astype(bf16)
    src = lax.broadcasted_iota(jnp.int32, (256, 256), 0)
    dst = lax.broadcasted_iota(jnp.int32, (256, 256), 1)
    wanted = (dst % 128 // 32) * 64 + (dst // 128) * 32 + dst % 32
    sorting = jnp.where(src == wanted, 1.0, 0.0).astype(bf16)
    for block in range(features // 256):
        columns = routed[:, block * 256 : (block + 1) * 256]
        columns = jnp.dot(columns, sorting, preferred_element_type=f32).astype(bf16)
        placed = jnp.dot(placing, columns, preferred_element_type=f32)
        for e in range(experts):
            piece = placed[e * capacity : (e + 1) * capacity].astype(bf16)
            for core in range(2):
                out_ref[2 * e + core, :, block * 128 : (block + 1) * 128] = piece[
                    :, core * 128 : (core + 1) * 128
                ]


def partial_kernel(chunk_ref, rows_ref, hidden_ref, up_ref, down_ref, middle_ref, part_ref):
    _, size, _ = part_ref.shape
    hidden = hidden_ref[...]
    for block in range(rows_ref.shape[1] // 256):
        part = lax.dot_general(
            rows_ref[:, block * 256 : (block + 1) * 256],
            hidden,
            (((0,), (0,)), ((), ())),
            preferred_element_type=jnp.float32,
        )
        for k in range(256 // size):
            part_ref[block * (256 // size) + k] = part[k * size : (k + 1) * size]
    at = 0
    for ref in (up_ref, down_ref, middle_ref):
        for i in range(ref.shape[0]):
            ref[i] = part_ref[chunk_ref[at]].astype(ref.dtype)
            at += 1


def newton_kernel(velocity_ref, own_ref, other_ref, out_ref, gram_ref):
    f32, bf16 = jnp.float32, jnp.bfloat16
    units = own_ref.shape[0]
    rows = velocity_ref.shape[0]
    trace = jnp.zeros((1, 128), f32)
    eye = lax.broadcasted_iota(jnp.int32, (128, 128), 0) == lax.broadcasted_iota(
        jnp.int32, (128, 128), 1
    )
    for i in range(units // 128):
        at = slice(i * 128, (i + 1) * 128)
        tile = own_ref[at, at] + other_ref[at, at].astype(f32)
        trace = trace + jnp.sum(jnp.where(eye, tile, 0.0), axis=0, keepdims=True)
    square_sum = jnp.sum(trace, axis=1, keepdims=True) + EPSILON
    inverse = 1.0 / square_sum
    gram_ref[...] = ((own_ref[...] + other_ref[...].astype(f32)) * inverse).astype(bf16)
    gram = gram_ref[...]

    def times(x):
        high = x.astype(bf16)
        low = (x - high.astype(f32)).astype(bf16)
        both = jnp.dot(
            jnp.concatenate([high, low], axis=0), gram, preferred_element_type=f32
        )
        return both[:rows] + both[rows:]

    def apply_first(x):
        once = times(x)
        return QUINTIC[0] * x + QUINTIC[1] * once + QUINTIC[2] * times(once)

    def apply_second(x):
        return apply_first(times(apply_first(x)))

    start = velocity_ref[...] / jnp.sqrt(square_sum)
    first = apply_first(start)
    once_more = apply_second(first)
    twice_more = apply_second(once_more)
    final = QUINTIC[0] * first + QUINTIC[1] * once_more + QUINTIC[2] * twice_more
    out_ref[...] = final * jnp.sqrt(jnp.float32(D))


def after(x, earlier):
    return lax.optimization_barrier((x, earlier))[0]


def reduce_over_ring(up, down, middle, ring):
    f32, bf16 = jnp.float32, jnp.bfloat16
    up = shifted(up, -1, ring)
    down = shifted(down, 1, ring)
    sums = {}
    for n, a in enumerate(FAR):
        sums[a] = middle[n] + down[DOWN.index(a)].astype(f32)
        if a in UP:
            sums[a] = sums[a] + up[UP.index(a)].astype(f32)
    sums = lax.optimization_barrier(sums)
    got = {}
    last = None
    for k in range(REACH, 0, -1):
        for side in (1, -1):
            total = sums[side * k]
            if side in got:
                total = total + after(got[side], last).astype(f32)
            last = total.astype(bf16 if k in NARROW else f32)
            got[side] = shifted(last, -side * STRIDE, ring)
    return sums[0] + got[1].astype(f32) + got[-1].astype(f32)


def gram_of(blocks):
    flat = blocks.reshape(-1, blocks.shape[-1])
    return lax.dot_general(
        flat, flat, (((0,), (0,)), ((), ())), preferred_element_type=jnp.float32
    )


def gram_over_ring(own, ring):
    held = {0: own}
    for k in range(1, REACH + 1):
        for side in (1, -1):
            held[side * k] = shifted(held[side * (k - 1)], -side * STRIDE, ring)
    rows = jnp.stack([held[a] for a in FAR])
    up = shifted(rows[: len(UP)], -1, ring)
    down = shifted(rows, 1, ring)
    return gram_of(rows) + gram_of(up) + gram_of(down)


def local(out_grad, expert_ids, route_gates, hidden_saved, momentum):
    f32, bf16 = jnp.float32, jnp.bfloat16
    n_expert = lax.axis_size("expert")
    ring = lax.axis_size("z")
    z = lax.axis_index("z")
    core = lax.axis_index("core")
    _, d_local, units = momentum.shape
    tok_rows, features = out_grad.shape
    capacity = hidden_saved.shape[3]
    half = features // 2
    own_hidden = hidden_saved.reshape(n_expert, capacity, units)
    other_hidden = swapped(own_hidden)
    outgoing = pl.pallas_call(
        lambda *refs: route_kernel(*refs, experts=n_expert, capacity=capacity),
        out_shape=jax.ShapeDtypeStruct((2 * n_expert, capacity, half), bf16),
        name="route",
    )(expert_ids.reshape(1, tok_rows), route_gates.reshape(1, tok_rows), out_grad)
    received = lax.all_to_all(
        outgoing, ("expert", "core"), split_axis=0, concat_axis=0, tiled=True
    )
    rows = received.reshape(2 * n_expert * capacity, half)
    first_core = core == 0
    hidden = jnp.stack(
        [
            jnp.where(first_core, own_hidden, other_hidden),
            jnp.where(first_core, other_hidden, own_hidden),
        ],
        axis=1,
    ).reshape(2 * n_expert * capacity, units)
    chunk = (z - jnp.array(OFFSETS, dtype=jnp.int32)) % ring
    up, down, middle = pl.pallas_call(
        partial_kernel,
        out_shape=(
            jax.ShapeDtypeStruct((len(UP), d_local, units), bf16),
            jax.ShapeDtypeStruct((len(DOWN), d_local, units), bf16),
            jax.ShapeDtypeStruct((len(FAR), d_local, units), f32),
        ),
        in_specs=[
            pl.BlockSpec(memory_space=pltpu.SMEM),
            pl.BlockSpec(memory_space=pltpu.VMEM),
            pl.BlockSpec(memory_space=pltpu.VMEM),
        ],
        out_specs=(
            pl.BlockSpec(memory_space=pltpu.VMEM),
            pl.BlockSpec(memory_space=pltpu.VMEM),
            pl.BlockSpec(memory_space=pltpu.VMEM),
        ),
        scratch_shapes=[pltpu.VMEM((ring, d_local, units), f32)],
        name="partial",
    )(chunk, rows, hidden)
    gradient = reduce_over_ring(up, down, middle, ring)
    moment_new = DECAY * momentum[0] + gradient
    velocity = gradient + DECAY * moment_new
    gram = gram_over_ring(velocity.astype(bf16), ring)
    other_gram = swapped(gram.astype(bf16))
    update = pl.pallas_call(
        newton_kernel,
        out_shape=jax.ShapeDtypeStruct((d_local, units), f32),
        scratch_shapes=[pltpu.VMEM((units, units), bf16)],
        name="newton",
    )(velocity, gram, other_gram)
    return moment_new[None], update[None]


def solution(mesh):
    finer = Mesh(
        mesh.devices.reshape(mesh.shape["expert"], mesh.shape["fsdp"] // 2, 2), EXPERT_FSDP
    )
    placed = (
        P(EXPERT_FSDP, None),
        P(EXPERT_FSDP, None),
        P(EXPERT_FSDP, None),
        P("expert", FSDP, None, None, None),
        P("expert", FSDP, None),
    )
    return jax.shard_map(
        local,
        mesh=finer,
        in_specs=placed,
        out_specs=(P("expert", FSDP, None), P("expert", FSDP, None)),
        check_vma=False,
    )
```

time: 689 us -> 231 us (0.34)
  waiting for transfers between devices: 598 us -> 63.1 us
  starting transfers between devices: 0.3 us -> 138 us
  blocking collectives: 22.2 us -> 0 us
  matrix products: 25 us -> 3.89 us
  local copies, waits for them, and re-layouts: 23.9 us -> 3.42 us
  Pallas kernels: 0 us -> 14.7 us
  between operations: 15.1 us -> 1.15 us
    psum x1 -> x0, waiting for transfers between devices: 426 us -> none  [local(): summed_tiles = lax.psum(packed, FSDP)]
    reduce_scatter x2 -> x0, waiting for transfers between devices: 172 us -> none  [reduced_to_own(): pieces = lax.psum_scatter(pieces, axes[k], scatter_dimension=0, tiled=True)]
    ppermute x0 -> x26, starting transfers between devices: none -> 120 us  [the longest x24 100 us: shifted(): return lax.ppermute(x, 'z', [(i, (i + by) % ring) for i in range(ring)])]
    ppermute x0 -> x26, waiting for transfers between devices: none -> 45.9 us  [the longest x24 42.4 us: shifted(): return lax.ppermute(x, 'z', [(i, (i + by) % ring) for i in range(ring)])]
    all_to_all x1 -> x0, blocking collectives: 22.2 us -> none  [local(): lax.all_to_all(outgoing, 'expert', split_axis=0, concat_axis=0, tiled=True)]
    dot_general x15 -> x3, matrix products: 25 us -> 3.89 us  [gram_of(): lax.dot_general(flat, flat, (((0,), (0,)), ((), ())), preferred_element_t...]
    all_to_all x0 -> x1, starting transfers between devices: none -> 17.9 us  [local(): lax.all_to_all(outgoing, ('expert', 'core'), split_axis=0, concat_axis=0,...]
    all_to_all x0 -> x1, waiting for transfers between devices: none -> 17.1 us  [local(): lax.all_to_all(outgoing, ('expert', 'core'), split_axis=0, concat_axis=0,...]
  transfers between devices with their start and end apart: 3 -> 27, of which waited for: 3 -> 14; matrix products, arithmetic and copies ran while one was open for 0% -> 1% of each run, Pallas kernels for 0% -> 0%
where the time goes in v1:
time: 231 us; the launch traced here: 228 us
  starting transfers between devices  138 us (60%)
  waiting for transfers between devices  63.1 us (27%)
  Pallas kernels  14.7 us (6%)
  matrix products  3.89 us (2%)
  other arithmetic  3.59 us (2%)
  local copies, waits for them, and re-layouts  3.42 us (1%)
    ppermute x24, starting transfers between devices, shifted(): return lax.ppermute(x, 'z', [(i, (i + by) % ring) for i in range(ring)])  100 us
    ppermute x24, waiting for transfers between devices, shifted(): return lax.ppermute(x, 'z', [(i, (i + by) % ring) for i in range(ring)])  42.4 us
    ppermute x2, starting transfers between devices, swapped(): return lax.ppermute(x, 'core', [(0, 1), (1, 0)])  19.8 us
    all_to_all x1, starting transfers between devices, local(): lax.all_to_all(outgoing, ('expert', 'core'), split_axis=0, concat_axis=0,...  17.9 us
    all_to_all x1, waiting for transfers between devices, local(): lax.all_to_all(outgoing, ('expert', 'core'), split_axis=0, concat_axis=0,...  17.1 us
    pallas_call x1, Pallas kernels, local(): pl.pallas_call(newton_kernel, out_shape=jax.ShapeDtypeStruct((d_local, un...  5.92 us
    pallas_call x1, Pallas kernels, local(): pl.pallas_call(partial_kernel, out_shape=(jax.ShapeDtypeStruct((len(UP),...  4.62 us
  transfers between devices with their start and end apart: 27, of which 14 were waited for; matrix products, arithmetic and copies ran while one was open for 1% of the time, Pallas kernels for 0%

profile of v1, /device:TPU:1, one launch (start us, length us, event | category | flops | bytes accessed | tf_op | source)
XLA Modules:
  0.0 227.8 jit_solution(17127944857417520547)
XLA Ops:
  0.6 4.2 %route.1 = bf16[32,24,1024]{2,1,0:T(8,128)(2,1)} custom-call(s32[1,256]{1,0:T(1,128)} %bitcast.93, f32[1,256]{1,0:T(1,128)} %bitcast.94, bf16[256,2048]{1,0:T(8,128)(2,1)} %refs_2_.1), custom_call_target="tpu_custom_call" | custom-call | tf_op jit(solution)/shard_map/route/pallas_call | solution.py:186
  4.8 17.9 %all-to-all-start = ((bf16[32,24,1024]{2,1,0:T(8,128)(2,1)}), bf16[32,24,1024]{2,1,0:T(8,128)(2,1)S(1)}, u32[]{:S(2)}, u32[]{:S(2)}) async-start(bf16[32,24,1024]{2,1,0:T(8,128)(2,1)} %route.1), calls=%async_computation | async-start | bytes 3145728 | tf_op jit(solution)/shard_map/all_to_all | solution.py:191
  22.7 2.3 collective-permute-start
  27.9 17.1 %all-to-all-done = bf16[32,24,1024]{2,1,0:T(8,128)(2,1)S(1)} async-done(((bf16[32,24,1024]{2,1,0:T(8,128)(2,1)}), bf16[32,24,1024]{2,1,0:T(8,128)(2,1)S(1)}, u32[]{:S(2)}, u32[]{:S(2)}) %all-to-all-start) | async-done | bytes 1572896 | tf_op jit(solution)/shard_map/all_to_all | solution.py:191
  46.2 4.6 %partial.1 = (bf16[10,32,768]{2,1,0:T(8,128)(2,1)}, bf16[11,32,768]{2,1,0:T(8,128)(2,1)}, f32[11,32,768]{2,1,0:T(8,128)}) custom-call(s32[32]{0:T(128)} %and_select_fusion.chunk_ref, bf16[768,1024]{1,0:T(8,128)(2,1)} %bitcast.89, bf16[768,768]{1,0:T(8,128)(2,1)} %bitcast.90), custom_call_target="tpu_custom_call" | custom-call | tf_op jit(solution)/shard_map/partial/pallas_call | solution.py:204
  50.8 2.0 collective-permute-start.1
  52.9 9.1 %collective-permute-start.2 = (bf16[10,32,768]{2,1,0:T(8,128)(2,1)}, bf16[10,32,768]{2,1,0:T(8,128)(2,1)S(1)}, u32[]{:S(2)}, u32[]{:S(2)}) collective-permute-start(bf16[10,32,768]{2,1,0:T(8,128)(2,1)} %get-tuple-element.26), channel_id=1, source_target_pairs={{0,62},{2,0},{4,2},{6,4},{8,6},{10,8},{12,10},{14,12},{16,14},{18,... | collective-permute-start | bytes 1474568 | tf_op jit(solution)/shard_map/ppermute | solution.py:31
  62.0 8.9 %collective-permute-done.2 = bf16[10,32,768]{2,1,0:T(8,128)(2,1)S(1)} collective-permute-done((bf16[10,32,768]{2,1,0:T(8,128)(2,1)}, bf16[10,32,768]{2,1,0:T(8,128)(2,1)S(1)}, u32[]{:S(2)}, u32[]{:S(2)}) %collective-permute-start.2) | collective-permute-done | bytes 491552 | tf_op jit(solution)/shard_map/ppermute | solution.py:31
  73.1 5.3 %collective-permute-start.3 = (bf16[32,768]{1,0:T(8,128)(2,1)S(1)}, bf16[32,768]{1,0:T(8,128)(2,1)S(1)}, u32[]{:S(2)}, u32[]{:S(2)}) collective-permute-start(bf16[32,768]{1,0:T(8,128)(2,1)S(1)} %get-tuple-element.32), channel_id=1, source_target_pairs={{0,58},{2,60},{4,62},{6,0},{8,2},{10,4},{12,6},{14,8},{16,10},{18,... | collective-permute-start | bytes 147464 | tf_op jit(solution)/shard_map/ppermute | solution.py:31
  78.4 1.9 collective-permute-start.5
  80.3 6.4 %collective-permute-start.4 = (bf16[32,768]{1,0:T(8,128)(2,1)S(1)}, bf16[32,768]{1,0:T(8,128)(2,1)S(1)}, u32[]{:S(2)}, u32[]{:S(2)}) collective-permute-start(bf16[32,768]{1,0:T(8,128)(2,1)S(1)} %add_convert_fusion.1), channel_id=1, source_target_pairs={{0,58},{2,60},{4,62},{6,0},{8,2},{10,4},{12,6},{14,8},{16,10},{18,... | collective-permute-start | bytes 147464 | tf_op jit(solution)/shard_map/ppermute | solution.py:31
  86.7 1.9 collective-permute-start.7
  88.7 6.4 %collective-permute-start.6 = (f32[32,768]{1,0:T(8,128)S(1)}, f32[32,768]{1,0:T(8,128)S(1)}, u32[]{:S(2)}, u32[]{:S(2)}) collective-permute-start(f32[32,768]{1,0:T(8,128)S(1)} %convert_add_fusion.1), channel_id=1, source_target_pairs={{0,58},{2,60},{4,62},{6,0},{8,2},{10,4},{12,6},{14,8},{16,10},{18,... | collective-permute-start | bytes 294920 | tf_op jit(solution)/shard_map/ppermute | solution.py:31
  95.1 1.9 collective-permute-start.9
  97.1 7.7 %collective-permute-start.8 = (f32[32,768]{1,0:T(8,128)S(1)}, f32[32,768]{1,0:T(8,128)S(1)}, u32[]{:S(2)}, u32[]{:S(2)}) collective-permute-start(f32[32,768]{1,0:T(8,128)S(1)} %add.191), channel_id=1, source_target_pairs={{0,58},{2,60},{4,62},{6,0},{8,2},{10,4},{12,6},{14,8},{16,10},{18,... | collective-permute-start | bytes 294920 | tf_op jit(solution)/shard_map/ppermute | solution.py:31
  104.8 1.9 collective-permute-start.11
  108.4 6.6 %collective-permute-done.11 = f32[32,768]{1,0:T(8,128)S(1)} collective-permute-done((f32[32,768]{1,0:T(8,128)S(1)}, f32[32,768]{1,0:T(8,128)S(1)}, u32[]{:S(2)}, u32[]{:S(2)}) %collective-permute-start.11) | collective-permute-done | bytes 98336 | tf_op jit(solution)/shard_map/ppermute | solution.py:31
  115.0 1.9 collective-permute-start.12
  116.9 6.4 %collective-permute-start.10 = (f32[32,768]{1,0:T(8,128)S(1)}, f32[32,768]{1,0:T(8,128)S(1)}, u32[]{:S(2)}, u32[]{:S(2)}) collective-permute-start(f32[32,768]{1,0:T(8,128)S(1)} %add.193), channel_id=1, source_target_pairs={{0,58},{2,60},{4,62},{6,0},{8,2},{10,4},{12,6},{14,8},{16,10},{18,... | collective-permute-start | bytes 294920 | tf_op jit(solution)/shard_map/ppermute | solution.py:31
  125.6 2.5 %collective-permute-start.13 = (bf16[32,768]{1,0:T(8,128)(2,1)S(1)}, bf16[32,768]{1,0:T(8,128)(2,1)S(1)}, u32[]{:S(2)}, u32[]{:S(2)}) collective-permute-start(bf16[32,768]{1,0:T(8,128)(2,1)S(1)} %get-tuple-element.46), channel_id=1, source_target_pairs={{0,6},{2,8},{4,10},{6,12},{8,14},{10,16},{12,18},{14,20},{16,22},{... | collective-permute-start | bytes 147464 | tf_op jit(solution)/shard_map/ppermute | solution.py:31
  128.2 7.0 %collective-permute-done.13 = bf16[32,768]{1,0:T(8,128)(2,1)S(1)} collective-permute-done((bf16[32,768]{1,0:T(8,128)(2,1)S(1)}, bf16[32,768]{1,0:T(8,128)(2,1)S(1)}, u32[]{:S(2)}, u32[]{:S(2)}) %collective-permute-start.13) | collective-permute-done | bytes 49184 | tf_op jit(solution)/shard_map/ppermute | solution.py:31
  137.1 6.4 %collective-permute-start.18 = (bf16[32,768]{1,0:T(8,128)(2,1)S(1)}, bf16[32,768]{1,0:T(8,128)(2,1)S(1)}, u32[]{:S(2)}, u32[]{:S(2)}) collective-permute-start(bf16[32,768]{1,0:T(8,128)(2,1)S(1)} %get-tuple-element.46), channel_id=1, source_target_pairs={{0,58},{2,60},{4,62},{6,0},{8,2},{10,4},{12,6},{14,8},{16,10},{18,... | collective-permute-start | bytes 147464 | tf_op jit(solution)/shard_map/ppermute | solution.py:31
  145.5 6.4 %collective-permute-start.19 = (bf16[32,768]{1,0:T(8,128)(2,1)S(1)}, bf16[32,768]{1,0:T(8,128)(2,1)S(1)}, u32[]{:S(2)}, u32[]{:S(2)}) collective-permute-start(bf16[32,768]{1,0:T(8,128)(2,1)S(1)} %collective-permute-done.18), channel_id=1, source_target_pairs={{0,58},{2,60},{4,62},{6,0},{8,2},{10,4},{12,6},{14,8},{16,10},{18,... | collective-permute-start | bytes 147464 | tf_op jit(solution)/shard_map/ppermute | solution.py:31
  153.8 6.4 %collective-permute-start.20 = (bf16[32,768]{1,0:T(8,128)(2,1)S(1)}, bf16[32,768]{1,0:T(8,128)(2,1)S(1)}, u32[]{:S(2)}, u32[]{:S(2)}) collective-permute-start(bf16[32,768]{1,0:T(8,128)(2,1)S(1)} %collective-permute-done.19), channel_id=1, source_target_pairs={{0,58},{2,60},{4,62},{6,0},{8,2},{10,4},{12,6},{14,8},{16,10},{18,... | collective-permute-start | bytes 147464 | tf_op jit(solution)/shard_map/ppermute | solution.py:31
  162.6 6.4 %collective-permute-start.21 = (bf16[32,768]{1,0:T(8,128)(2,1)S(1)}, bf16[32,768]{1,0:T(8,128)(2,1)S(1)}, u32[]{:S(2)}, u32[]{:S(2)}) collective-permute-start(bf16[32,768]{1,0:T(8,128)(2,1)S(1)} %collective-permute-done.20), channel_id=1, source_target_pairs={{0,58},{2,60},{4,62},{6,0},{8,2},{10,4},{12,6},{14,8},{16,10},{18,... | collective-permute-start | bytes 147464 | tf_op jit(solution)/shard_map/ppermute | solution.py:31
  170.1 7.9 %collective-permute-start.23 = (bf16[10,32,768]{2,1,0:T(8,128)(2,1)S(1)}, bf16[10,32,768]{2,1,0:T(8,128)(2,1)S(1)}, u32[]{:S(2)}, u32[]{:S(2)}) collective-permute-start(bf16[10,32,768]{2,1,0:T(8,128)(2,1)S(1)} %get-tuple-element.62), channel_id=1, source_target_pairs={{0,62},{2,0},{4,2},{6,4},{8,6},{10,8},{12,10},{14,12},{16,14},{18,... | collective-permute-start | bytes 1474568 | tf_op jit(solution)/shard_map/ppermute | solution.py:31
  180.0 6.5 %collective-permute-done.22 = bf16[32,768]{1,0:T(8,128)(2,1)S(1)} collective-permute-done((bf16[32,768]{1,0:T(8,128)(2,1)S(1)}, bf16[32,768]{1,0:T(8,128)(2,1)S(1)}, u32[]{:S(2)}, u32[]{:S(2)}) %collective-permute-start.22) | collective-permute-done | bytes 49184 | tf_op jit(solution)/shard_map/ppermute | solution.py:31
  189.2 8.6 %collective-permute-done.24 = bf16[11,32,768]{2,1,0:T(8,128)(2,1)S(1)} collective-permute-done((bf16[11,32,768]{2,1,0:T(8,128)(2,1)S(1)}, bf16[11,32,768]{2,1,0:T(8,128)(2,1)S(1)}, u32[]{:S(2)}, u32[]{:S(2)}) %collective-permute-start.24) | collective-permute-done | bytes 540704 | tf_op jit(solution)/shard_map/ppermute | solution.py:31
  198.6 2.3 %fusion.3 = (bf16[768,768]{1,0:T(8,128)(2,1)S(1)}, f32[768,768]{1,0:T(8,128)}) fusion(f32[768,768,1]{1,0,2:T(8,128)S(1)} %fusion.5, f32[768,768,1]{1,0,2:T(8,128)S(1)} %fusion.4, bf16[11,32,768]{2,1,0:T(8,128)(2,1)S(1)} %bitcast_dynamic-update-slice_fusion), kind=kOutput, calls=%fused_computation.50 | convolution fusion | flops 417005568 | bytes 8798208 | tf_op jit(solution)/shard_map/dot_general | solution.py:158
  200.9 17.5 %collective-permute-start.25 = (bf16[768,768]{1,0:T(8,128)(2,1)S(1)}, bf16[768,768]{1,0:T(8,128)(2,1)S(1)}, u32[]{:S(2)}, u32[]{:S(2)}) collective-permute-start(bf16[768,768]{1,0:T(8,128)(2,1)S(1)} %get-tuple-element.82), channel_id=1, source_target_pairs={{0,1},{1,0},{2,3},{3,2},{4,5},{5,4},{6,7},{7,6},{8,9},{9,8},{10,11... | collective-permute-start | bytes 3538952 | tf_op jit(solution)/shard_map/ppermute | solution.py:35
  218.4 2.5 %collective-permute-done.25.other_ref = bf16[768,768]{1,0:T(8,128)(2,1)S(1)} collective-permute-done((bf16[768,768]{1,0:T(8,128)(2,1)S(1)}, bf16[768,768]{1,0:T(8,128)(2,1)S(1)}, u32[]{:S(2)}, u32[]{:S(2)}) %collective-permute-start.25) | collective-permute-done | bytes 1179680 | tf_op jit(solution)/shard_map/ppermute | solution.py:35
  221.9 5.9 %newton.1 = f32[32,768]{1,0:T(8,128)} custom-call(f32[32,768]{1,0:T(8,128)} %get-tuple-element.47.velocity_ref, f32[768,768]{1,0:T(8,128)} %get-tuple-element.83.own_ref, bf16[768,768]{1,0:T(8,128)(2,1)} %copy-done.1), custom_call_target="tpu_custom_call" | custom-call | tf_op jit(solution)/shard_map/newton/pallas_call | solution.py:229
  (67 shorter events, 26.1 us)
Async XLA Ops:
  4.8 17.9 %copy-start.3 = (bf16[1,1,16,24,768]{4,3,2,1,0:T(8,128)(2,1)S(1)}, bf16[1,1,16,24,768]{4,3,2,1,0:T(8,128)(2,1)}, u32[]{:S(2)}) copy-start(bf16[1,1,16,24,768]{4,3,2,1,0:T(8,128)(2,1)} %param.9) | copy-start | bytes 1769476
  4.8 20.2 %copy-start.5 = (s32[32]{0:T(128)S(1)}, s32[32]{0:T(128)}, u32[]{:S(2)}) copy-start(s32[32]{0:T(128)} %constant.34) | copy-start | bytes 388
  4.8 40.2 %all-to-all-start = ((bf16[32,24,1024]{2,1,0:T(8,128)(2,1)}), bf16[32,24,1024]{2,1,0:T(8,128)(2,1)S(1)}, u32[]{:S(2)}, u32[]{:S(2)}) async-start(bf16[32,24,1024]{2,1,0:T(8,128)(2,1)} %route.1), calls=%async_computation | async-start | bytes 3145728 | tf_op jit(solution)/shard_map/all_to_all | solution.py:191
  22.7 3.9 %collective-permute-start = (bf16[16,24,768]{2,1,0:T(8,128)(2,1)S(1)}, bf16[16,24,768]{2,1,0:T(8,128)(2,1)S(1)}, u32[]{:S(2)}, u32[]{:S(2)}) collective-permute-start(bf16[16,24,768]{2,1,0:T(8,128)(2,1)S(1)} %bitcast.91), channel_id=1, source_target_pairs={{0,1},{1,0},{2,3},{3,2},{4,5},{5,4},{6,7},{7,6},{8,9},{9,8},{10,11... | collective-permute-start | bytes 1769480 | tf_op jit(solution)/shard_map/ppermute | solution.py:35
  45.0 1.2 copy-start
  50.8 22.1 %copy-start.2 = (f32[11,32,768]{2,1,0:T(8,128)S(1)}, f32[11,32,768]{2,1,0:T(8,128)}, u32[]{:S(2)}) copy-start(f32[11,32,768]{2,1,0:T(8,128)} %get-tuple-element.24) | copy-start | bytes 3244036
  50.8 20.1 %collective-permute-start.1 = (bf16[11,32,768]{2,1,0:T(8,128)(2,1)}, bf16[11,32,768]{2,1,0:T(8,128)(2,1)S(1)}, u32[]{:S(2)}, u32[]{:S(2)}) collective-permute-start(bf16[11,32,768]{2,1,0:T(8,128)(2,1)} %get-tuple-element.25), channel_id=1, source_target_pairs={{0,2},{2,4},{4,6},{6,8},{8,10},{10,12},{12,14},{14,16},{16,18},{18... | collective-permute-start | bytes 1622024 | tf_op jit(solution)/shard_map/ppermute | solution.py:31
  52.9 18.0 %collective-permute-start.2 = (bf16[10,32,768]{2,1,0:T(8,128)(2,1)}, bf16[10,32,768]{2,1,0:T(8,128)(2,1)S(1)}, u32[]{:S(2)}, u32[]{:S(2)}) collective-permute-start(bf16[10,32,768]{2,1,0:T(8,128)(2,1)} %get-tuple-element.26), channel_id=1, source_target_pairs={{0,62},{2,0},{4,2},{6,4},{8,6},{10,8},{12,10},{14,12},{16,14},{18,... | collective-permute-start | bytes 1474568 | tf_op jit(solution)/shard_map/ppermute | solution.py:31
  73.0 52.0 %copy-start.4 = (f32[1,32,768]{2,1,0:T(8,128)S(1)}, f32[1,32,768]{2,1,0:T(8,128)}, u32[]{:S(2)}) copy-start(f32[1,32,768]{2,1,0:T(8,128)} %param.10) | copy-start | bytes 294916
  73.1 7.2 %collective-permute-start.3 = (bf16[32,768]{1,0:T(8,128)(2,1)S(1)}, bf16[32,768]{1,0:T(8,128)(2,1)S(1)}, u32[]{:S(2)}, u32[]{:S(2)}) collective-permute-start(bf16[32,768]{1,0:T(8,128)(2,1)S(1)} %get-tuple-element.32), channel_id=1, source_target_pairs={{0,58},{2,60},{4,62},{6,0},{8,2},{10,4},{12,6},{14,8},{16,10},{18,... | collective-permute-start | bytes 147464 | tf_op jit(solution)/shard_map/ppermute | solution.py:31
  78.4 8.3 %collective-permute-start.5 = (bf16[32,768]{1,0:T(8,128)(2,1)S(1)}, bf16[32,768]{1,0:T(8,128)(2,1)S(1)}, u32[]{:S(2)}, u32[]{:S(2)}) collective-permute-start(bf16[32,768]{1,0:T(8,128)(2,1)S(1)} %get-tuple-element.33), channel_id=1, source_target_pairs={{0,6},{2,8},{4,10},{6,12},{8,14},{10,16},{12,18},{14,20},{16,22},{... | collective-permute-start | bytes 147464 | tf_op jit(solution)/shard_map/ppermute | solution.py:31
  80.3 8.3 %collective-permute-start.4 = (bf16[32,768]{1,0:T(8,128)(2,1)S(1)}, bf16[32,768]{1,0:T(8,128)(2,1)S(1)}, u32[]{:S(2)}, u32[]{:S(2)}) collective-permute-start(bf16[32,768]{1,0:T(8,128)(2,1)S(1)} %add_convert_fusion.1), channel_id=1, source_target_pairs={{0,58},{2,60},{4,62},{6,0},{8,2},{10,4},{12,6},{14,8},{16,10},{18,... | collective-permute-start | bytes 147464 | tf_op jit(solution)/shard_map/ppermute | solution.py:31
  86.7 8.3 %collective-permute-start.7 = (bf16[32,768]{1,0:T(8,128)(2,1)S(1)}, bf16[32,768]{1,0:T(8,128)(2,1)S(1)}, u32[]{:S(2)}, u32[]{:S(2)}) collective-permute-start(bf16[32,768]{1,0:T(8,128)(2,1)S(1)} %add_convert_fusion), channel_id=1, source_target_pairs={{0,6},{2,8},{4,10},{6,12},{8,14},{10,16},{12,18},{14,20},{16,22},{... | collective-permute-start | bytes 147464 | tf_op jit(solution)/shard_map/ppermute | solution.py:31
  88.7 8.3 %collective-permute-start.6 = (f32[32,768]{1,0:T(8,128)S(1)}, f32[32,768]{1,0:T(8,128)S(1)}, u32[]{:S(2)}, u32[]{:S(2)}) collective-permute-start(f32[32,768]{1,0:T(8,128)S(1)} %convert_add_fusion.1), channel_id=1, source_target_pairs={{0,58},{2,60},{4,62},{6,0},{8,2},{10,4},{12,6},{14,8},{16,10},{18,... | collective-permute-start | bytes 294920 | tf_op jit(solution)/shard_map/ppermute | solution.py:31
  95.1 9.7 %collective-permute-start.9 = (f32[32,768]{1,0:T(8,128)S(1)}, f32[32,768]{1,0:T(8,128)S(1)}, u32[]{:S(2)}, u32[]{:S(2)}) collective-permute-start(f32[32,768]{1,0:T(8,128)S(1)} %convert_add_fusion), channel_id=1, source_target_pairs={{0,6},{2,8},{4,10},{6,12},{8,14},{10,16},{12,18},{14,20},{16,22},{... | collective-permute-start | bytes 294920 | tf_op jit(solution)/shard_map/ppermute | solution.py:31
  97.1 11.4 %collective-permute-start.8 = (f32[32,768]{1,0:T(8,128)S(1)}, f32[32,768]{1,0:T(8,128)S(1)}, u32[]{:S(2)}, u32[]{:S(2)}) collective-permute-start(f32[32,768]{1,0:T(8,128)S(1)} %add.191), channel_id=1, source_target_pairs={{0,58},{2,60},{4,62},{6,0},{8,2},{10,4},{12,6},{14,8},{16,10},{18,... | collective-permute-start | bytes 294920 | tf_op jit(solution)/shard_map/ppermute | solution.py:31
  104.8 10.2 %collective-permute-start.11 = (f32[32,768]{1,0:T(8,128)S(1)}, f32[32,768]{1,0:T(8,128)S(1)}, u32[]{:S(2)}, u32[]{:S(2)}) collective-permute-start(f32[32,768]{1,0:T(8,128)S(1)} %add.192), channel_id=1, source_target_pairs={{0,6},{2,8},{4,10},{6,12},{8,14},{10,16},{12,18},{14,20},{16,22},{... | collective-permute-start | bytes 294920 | tf_op jit(solution)/shard_map/ppermute | solution.py:31
  115.0 8.5 %collective-permute-start.12 = (f32[32,768]{1,0:T(8,128)S(1)}, f32[32,768]{1,0:T(8,128)S(1)}, u32[]{:S(2)}, u32[]{:S(2)}) collective-permute-start(f32[32,768]{1,0:T(8,128)S(1)} %add.195), channel_id=1, source_target_pairs={{0,6},{2,8},{4,10},{6,12},{8,14},{10,16},{12,18},{14,20},{16,22},{... | collective-permute-start | bytes 294920 | tf_op jit(solution)/shard_map/ppermute | solution.py:31
  116.9 8.0 %collective-permute-start.10 = (f32[32,768]{1,0:T(8,128)S(1)}, f32[32,768]{1,0:T(8,128)S(1)}, u32[]{:S(2)}, u32[]{:S(2)}) collective-permute-start(f32[32,768]{1,0:T(8,128)S(1)} %add.193), channel_id=1, source_target_pairs={{0,58},{2,60},{4,62},{6,0},{8,2},{10,4},{12,6},{14,8},{16,10},{18,... | collective-permute-start | bytes 294920 | tf_op jit(solution)/shard_map/ppermute | solution.py:31
  125.6 9.5 %collective-permute-start.13 = (bf16[32,768]{1,0:T(8,128)(2,1)S(1)}, bf16[32,768]{1,0:T(8,128)(2,1)S(1)}, u32[]{:S(2)}, u32[]{:S(2)}) collective-permute-start(bf16[32,768]{1,0:T(8,128)(2,1)S(1)} %get-tuple-element.46), channel_id=1, source_target_pairs={{0,6},{2,8},{4,10},{6,12},{8,14},{10,16},{12,18},{14,20},{16,22},{... | collective-permute-start | bytes 147464 | tf_op jit(solution)/shard_map/ppermute | solution.py:31
  135.1 8.4 %collective-permute-start.14 = (bf16[32,768]{1,0:T(8,128)(2,1)S(1)}, bf16[32,768]{1,0:T(8,128)(2,1)S(1)}, u32[]{:S(2)}, u32[]{:S(2)}) collective-permute-start(bf16[32,768]{1,0:T(8,128)(2,1)S(1)} %collective-permute-done.13), channel_id=1, source_target_pairs={{0,6},{2,8},{4,10},{6,12},{8,14},{10,16},{12,18},{14,20},{16,22},{... | collective-permute-start | bytes 147464 | tf_op jit(solution)/shard_map/ppermute | solution.py:31
  137.1 8.4 %collective-permute-start.18 = (bf16[32,768]{1,0:T(8,128)(2,1)S(1)}, bf16[32,768]{1,0:T(8,128)(2,1)S(1)}, u32[]{:S(2)}, u32[]{:S(2)}) collective-permute-start(bf16[32,768]{1,0:T(8,128)(2,1)S(1)} %get-tuple-element.46), channel_id=1, source_target_pairs={{0,58},{2,60},{4,62},{6,0},{8,2},{10,4},{12,6},{14,8},{16,10},{18,... | collective-permute-start | bytes 147464 | tf_op jit(solution)/shard_map/ppermute | solution.py:31
  143.6 8.3 %collective-permute-start.15 = (bf16[32,768]{1,0:T(8,128)(2,1)S(1)}, bf16[32,768]{1,0:T(8,128)(2,1)S(1)}, u32[]{:S(2)}, u32[]{:S(2)}) collective-permute-start(bf16[32,768]{1,0:T(8,128)(2,1)S(1)} %collective-permute-done.14), channel_id=1, source_target_pairs={{0,6},{2,8},{4,10},{6,12},{8,14},{10,16},{12,18},{14,20},{16,22},{... | collective-permute-start | bytes 147464 | tf_op jit(solution)/shard_map/ppermute | solution.py:31
  145.5 8.3 %collective-permute-start.19 = (bf16[32,768]{1,0:T(8,128)(2,1)S(1)}, bf16[32,768]{1,0:T(8,128)(2,1)S(1)}, u32[]{:S(2)}, u32[]{:S(2)}) collective-permute-start(bf16[32,768]{1,0:T(8,128)(2,1)S(1)} %collective-permute-done.18), channel_id=1, source_target_pairs={{0,58},{2,60},{4,62},{6,0},{8,2},{10,4},{12,6},{14,8},{16,10},{18,... | collective-permute-start | bytes 147464 | tf_op jit(solution)/shard_map/ppermute | solution.py:31
  151.9 8.7 %collective-permute-start.16 = (bf16[32,768]{1,0:T(8,128)(2,1)S(1)}, bf16[32,768]{1,0:T(8,128)(2,1)S(1)}, u32[]{:S(2)}, u32[]{:S(2)}) collective-permute-start(bf16[32,768]{1,0:T(8,128)(2,1)S(1)} %collective-permute-done.15), channel_id=1, source_target_pairs={{0,6},{2,8},{4,10},{6,12},{8,14},{10,16},{12,18},{14,20},{16,22},{... | collective-permute-start | bytes 147464 | tf_op jit(solution)/shard_map/ppermute | solution.py:31
  153.8 8.7 %collective-permute-start.20 = (bf16[32,768]{1,0:T(8,128)(2,1)S(1)}, bf16[32,768]{1,0:T(8,128)(2,1)S(1)}, u32[]{:S(2)}, u32[]{:S(2)}) collective-permute-start(bf16[32,768]{1,0:T(8,128)(2,1)S(1)} %collective-permute-done.19), channel_id=1, source_target_pairs={{0,58},{2,60},{4,62},{6,0},{8,2},{10,4},{12,6},{14,8},{16,10},{18,... | collective-permute-start | bytes 147464 | tf_op jit(solution)/shard_map/ppermute | solution.py:31
  160.7 8.3 %collective-permute-start.17 = (bf16[32,768]{1,0:T(8,128)(2,1)S(1)}, bf16[32,768]{1,0:T(8,128)(2,1)S(1)}, u32[]{:S(2)}, u32[]{:S(2)}) collective-permute-start(bf16[32,768]{1,0:T(8,128)(2,1)S(1)} %collective-permute-done.16), channel_id=1, source_target_pairs={{0,6},{2,8},{4,10},{6,12},{8,14},{10,16},{12,18},{14,20},{16,22},{... | collective-permute-start | bytes 147464 | tf_op jit(solution)/shard_map/ppermute | solution.py:31
  162.6 7.5 %collective-permute-start.21 = (bf16[32,768]{1,0:T(8,128)(2,1)S(1)}, bf16[32,768]{1,0:T(8,128)(2,1)S(1)}, u32[]{:S(2)}, u32[]{:S(2)}) collective-permute-start(bf16[32,768]{1,0:T(8,128)(2,1)S(1)} %collective-permute-done.20), channel_id=1, source_target_pairs={{0,58},{2,60},{4,62},{6,0},{8,2},{10,4},{12,6},{14,8},{16,10},{18,... | collective-permute-start | bytes 147464 | tf_op jit(solution)/shard_map/ppermute | solution.py:31
  170.1 18.3 %collective-permute-start.23 = (bf16[10,32,768]{2,1,0:T(8,128)(2,1)S(1)}, bf16[10,32,768]{2,1,0:T(8,128)(2,1)S(1)}, u32[]{:S(2)}, u32[]{:S(2)}) collective-permute-start(bf16[10,32,768]{2,1,0:T(8,128)(2,1)S(1)} %get-tuple-element.62), channel_id=1, source_target_pairs={{0,62},{2,0},{4,2},{6,4},{8,6},{10,8},{12,10},{14,12},{16,14},{18,... | collective-permute-start | bytes 1474568 | tf_op jit(solution)/shard_map/ppermute | solution.py:31
  178.1 8.4 %collective-permute-start.22 = (bf16[32,768]{1,0:T(8,128)(2,1)S(1)}, bf16[32,768]{1,0:T(8,128)(2,1)S(1)}, u32[]{:S(2)}, u32[]{:S(2)}) collective-permute-start(bf16[32,768]{1,0:T(8,128)(2,1)S(1)} %collective-permute-done.21), channel_id=1, source_target_pairs={{0,58},{2,60},{4,62},{6,0},{8,2},{10,4},{12,6},{14,8},{16,10},{18,... | collective-permute-start | bytes 147464 | tf_op jit(solution)/shard_map/ppermute | solution.py:31
  186.5 11.3 %collective-permute-start.24 = (bf16[11,32,768]{2,1,0:T(8,128)(2,1)S(1)}, bf16[11,32,768]{2,1,0:T(8,128)(2,1)S(1)}, u32[]{:S(2)}, u32[]{:S(2)}) collective-permute-start(bf16[11,32,768]{2,1,0:T(8,128)(2,1)S(1)} %bitcast_dynamic-update-slice_fusion), channel_id=1, source_target_pairs={{0,2},{2,4},{4,6},{6,8},{8,10},{10,12},{12,14},{14,16},{16,18},{18... | collective-permute-start | bytes 1622024 | tf_op jit(solution)/shard_map/ppermute | solution.py:31
  200.9 20.0 %collective-permute-start.25 = (bf16[768,768]{1,0:T(8,128)(2,1)S(1)}, bf16[768,768]{1,0:T(8,128)(2,1)S(1)}, u32[]{:S(2)}, u32[]{:S(2)}) collective-permute-start(bf16[768,768]{1,0:T(8,128)(2,1)S(1)} %get-tuple-element.82), channel_id=1, source_target_pairs={{0,1},{1,0},{2,3},{3,2},{4,5},{5,4},{6,7},{7,6},{8,9},{9,8},{10,11... | collective-permute-start | bytes 3538952 | tf_op jit(solution)/shard_map/ppermute | solution.py:35
  (1 other events, 1.0 us)

commit v2 on v1

--- a/solution.py
+++ b/solution.py
@@ -24,8 +24,6 @@
     + tuple(STRIDE * a - 1 for a in DOWN)
     + tuple(STRIDE * a for a in FAR)
 )
-NARROW = (5, 4)
-
 
 def shifted(x, by, ring):
     return lax.ppermute(x, "z", [(i, (i + by) % ring) for i in range(ring)])
@@ -97,11 +95,12 @@
     )
     for i in range(units // 128):
         at = slice(i * 128, (i + 1) * 128)
-        tile = own_ref[at, at] + other_ref[at, at].astype(f32)
+        tile = own_ref[at, at].astype(f32) + other_ref[at, at].astype(f32)
         trace = trace + jnp.sum(jnp.where(eye, tile, 0.0), axis=0, keepdims=True)
     square_sum = jnp.sum(trace, axis=1, keepdims=True) + EPSILON
     inverse = 1.0 / square_sum
-    gram_ref[...] = ((own_ref[...] + other_ref[...].astype(f32)) * inverse).astype(bf16)
+    whole = own_ref[...].astype(f32) + other_ref[...].astype(f32)
+    gram_ref[...] = (whole * inverse).astype(bf16)
     gram = gram_ref[...]
 
     def times(x):
@@ -132,7 +131,7 @@
 
 
 def reduce_over_ring(up, down, middle, ring):
-    f32, bf16 = jnp.float32, jnp.bfloat16
+    f32 = jnp.float32
     up = shifted(up, -1, ring)
     down = shifted(down, 1, ring)
     sums = {}
@@ -147,10 +146,10 @@
         for side in (1, -1):
             total = sums[side * k]
             if side in got:
-                total = total + after(got[side], last).astype(f32)
-            last = total.astype(bf16 if k in NARROW else f32)
-            got[side] = shifted(last, -side * STRIDE, ring)
-    return sums[0] + got[1].astype(f32) + got[-1].astype(f32)
+                total = total + after(got[side], last)
+            last = total
+            got[side] = shifted(total, -side * STRIDE, ring)
+    return sums[0] + got[1] + got[-1]
 
 
 def gram_of(blocks):
@@ -165,7 +164,7 @@
     for k in range(1, REACH + 1):
         for side in (1, -1):
             held[side * k] = shifted(held[side * (k - 1)], -side * STRIDE, ring)
-    rows = jnp.stack([held[a] for a in FAR])
+    rows = lax.optimization_barrier(jnp.stack([held[a] for a in FAR]))
     up = shifted(rows[: len(UP)], -1, ring)
     down = shifted(rows, 1, ring)
     return gram_of(rows) + gram_of(up) + gram_of(down)
@@ -224,8 +223,8 @@
     gradient = reduce_over_ring(up, down, middle, ring)
     moment_new = DECAY * momentum[0] + gradient
     velocity = gradient + DECAY * moment_new
-    gram = gram_over_ring(velocity.astype(bf16), ring)
-    other_gram = swapped(gram.astype(bf16))
+    gram = gram_over_ring(velocity.astype(bf16), ring).astype(bf16)
+    other_gram = swapped(gram)
     update = pl.pallas_call(
         newton_kernel,
         out_shape=jax.ShapeDtypeStruct((d_local, units), f32),

time: 231 us -> 228 us (0.987)
  the two profiles are of different devices: /device:TPU:1 before, /device:TPU:9 now
where the time goes in v2:
time: 228 us; the launch traced here: 227 us
  starting transfers between devices  139 us (61%)
  waiting for transfers between devices  64 us (28%)
  Pallas kernels  14.4 us (6%)
  local copies, waits for them, and re-layouts  3.4 us (1%)
  other arithmetic  2.77 us (1%)
  matrix products  2.47 us (1%)
    ppermute x24, starting transfers between devices, shifted(): return lax.ppermute(x, 'z', [(i, (i + by) % ring) for i in range(ring)])  114 us
    ppermute x24, waiting for transfers between devices, shifted(): return lax.ppermute(x, 'z', [(i, (i + by) % ring) for i in range(ring)])  43.8 us
    all_to_all x1, starting transfers between devices, local(): lax.all_to_all(outgoing, ('expert', 'core'), split_axis=0, concat_axis=0,...  17.2 us
    all_to_all x1, waiting for transfers between devices, local(): lax.all_to_all(outgoing, ('expert', 'core'), split_axis=0, concat_axis=0,...  16.7 us
    ppermute x2, starting transfers between devices, swapped(): return lax.ppermute(x, 'core', [(0, 1), (1, 0)])  7.86 us
    pallas_call x1, Pallas kernels, local(): pl.pallas_call(newton_kernel, out_shape=jax.ShapeDtypeStruct((d_local, un...  5.63 us
    pallas_call x1, Pallas kernels, local(): pl.pallas_call(partial_kernel, out_shape=(jax.ShapeDtypeStruct((len(UP),...  4.63 us
  transfers between devices with their start and end apart: 27, of which 13 were waited for; matrix products, arithmetic and copies ran while one was open for 1% of the time, Pallas kernels for 0%

profile of v2, /device:TPU:9, one launch (start us, length us, event | category | flops | bytes accessed | tf_op | source)
XLA Modules:
  0.0 227.1 jit_solution(8542490394606301175)
XLA Ops:
  0.6 4.2 %route.1 = bf16[32,24,1024]{2,1,0:T(8,128)(2,1)} custom-call(s32[1,256]{1,0:T(1,128)} %bitcast.85, f32[1,256]{1,0:T(1,128)} %bitcast.86, bf16[256,2048]{1,0:T(8,128)(2,1)} %refs_2_.1), custom_call_target="tpu_custom_call" | custom-call | tf_op jit(solution)/shard_map/route/pallas_call | solution.py:185
  4.8 17.2 %all-to-all-start = ((bf16[32,24,1024]{2,1,0:T(8,128)(2,1)}), bf16[32,24,1024]{2,1,0:T(8,128)(2,1)S(1)}, u32[]{:S(2)}, u32[]{:S(2)}) async-start(bf16[32,24,1024]{2,1,0:T(8,128)(2,1)} %route.1), calls=%async_computation | async-start | bytes 3145728 | tf_op jit(solution)/shard_map/all_to_all | solution.py:190
  22.0 2.3 %collective-permute-start = (bf16[16,24,768]{2,1,0:T(8,128)(2,1)S(1)}, bf16[16,24,768]{2,1,0:T(8,128)(2,1)S(1)}, u32[]{:S(2)}, u32[]{:S(2)}) collective-permute-start(bf16[16,24,768]{2,1,0:T(8,128)(2,1)S(1)} %bitcast.83), channel_id=1, source_target_pairs={{0,1},{1,0},{2,3},{3,2},{4,5},{5,4},{6,7},{7,6},{8,9},{9,8},{10,11... | collective-permute-start | bytes 1769480 | tf_op jit(solution)/shard_map/ppermute | solution.py:33
  27.2 16.7 %all-to-all-done = bf16[32,24,1024]{2,1,0:T(8,128)(2,1)S(1)} async-done(((bf16[32,24,1024]{2,1,0:T(8,128)(2,1)}), bf16[32,24,1024]{2,1,0:T(8,128)(2,1)S(1)}, u32[]{:S(2)}, u32[]{:S(2)}) %all-to-all-start) | async-done | bytes 1572896 | tf_op jit(solution)/shard_map/all_to_all | solution.py:190
  45.1 4.6 %partial.1 = (bf16[10,32,768]{2,1,0:T(8,128)(2,1)}, bf16[11,32,768]{2,1,0:T(8,128)(2,1)}, f32[11,32,768]{2,1,0:T(8,128)}) custom-call(s32[32]{0:T(128)} %and_select_fusion.chunk_ref, bf16[768,1024]{1,0:T(8,128)(2,1)} %bitcast.81, bf16[768,768]{1,0:T(8,128)(2,1)} %bitcast.82), custom_call_target="tpu_custom_call" | custom-call | tf_op jit(solution)/shard_map/partial/pallas_call | solution.py:203
  49.7 2.0 collective-permute-start.1
  51.8 9.1 %collective-permute-start.2 = (bf16[10,32,768]{2,1,0:T(8,128)(2,1)}, bf16[10,32,768]{2,1,0:T(8,128)(2,1)S(1)}, u32[]{:S(2)}, u32[]{:S(2)}) collective-permute-start(bf16[10,32,768]{2,1,0:T(8,128)(2,1)} %get-tuple-element.26), channel_id=1, source_target_pairs={{0,62},{2,0},{4,2},{6,4},{8,6},{10,8},{12,10},{14,12},{16,14},{18,... | collective-permute-start | bytes 1474568 | tf_op jit(solution)/shard_map/ppermute | solution.py:29
  60.9 11.2 %collective-permute-done.2 = bf16[10,32,768]{2,1,0:T(8,128)(2,1)S(1)} collective-permute-done((bf16[10,32,768]{2,1,0:T(8,128)(2,1)}, bf16[10,32,768]{2,1,0:T(8,128)(2,1)S(1)}, u32[]{:S(2)}, u32[]{:S(2)}) %collective-permute-start.2) | collective-permute-done | bytes 491552 | tf_op jit(solution)/shard_map/ppermute | solution.py:29
  73.3 5.5 %collective-permute-start.3 = (f32[32,768]{1,0:T(8,128)S(1)}, f32[32,768]{1,0:T(8,128)S(1)}, u32[]{:S(2)}, u32[]{:S(2)}) collective-permute-start(f32[32,768]{1,0:T(8,128)S(1)} %get-tuple-element.32), channel_id=1, source_target_pairs={{0,58},{2,60},{4,62},{6,0},{8,2},{10,4},{12,6},{14,8},{16,10},{18,... | collective-permute-start | bytes 294920 | tf_op jit(solution)/shard_map/ppermute | solution.py:29
  78.8 1.9 collective-permute-start.5
  81.0 6.4 %collective-permute-start.4 = (f32[32,768]{1,0:T(8,128)S(1)}, f32[32,768]{1,0:T(8,128)S(1)}, u32[]{:S(2)}, u32[]{:S(2)}) collective-permute-start(f32[32,768]{1,0:T(8,128)S(1)} %add.187), channel_id=1, source_target_pairs={{0,58},{2,60},{4,62},{6,0},{8,2},{10,4},{12,6},{14,8},{16,10},{18,... | collective-permute-start | bytes 294920 | tf_op jit(solution)/shard_map/ppermute | solution.py:29
  87.4 1.9 collective-permute-done.5
  91.3 10.1 %collective-permute-start.6 = (f32[32,768]{1,0:T(8,128)S(1)}, f32[32,768]{1,0:T(8,128)S(1)}, u32[]{:S(2)}, u32[]{:S(2)}) collective-permute-start(f32[32,768]{1,0:T(8,128)S(1)} %add.189), channel_id=1, source_target_pairs={{0,58},{2,60},{4,62},{6,0},{8,2},{10,4},{12,6},{14,8},{16,10},{18,... | collective-permute-start | bytes 294920 | tf_op jit(solution)/shard_map/ppermute | solution.py:29
  103.4 4.5 %collective-permute-done.6 = f32[32,768]{1,0:T(8,128)S(1)} collective-permute-done((f32[32,768]{1,0:T(8,128)S(1)}, f32[32,768]{1,0:T(8,128)S(1)}, u32[]{:S(2)}, u32[]{:S(2)}) %collective-permute-start.6) | collective-permute-done | bytes 98336 | tf_op jit(solution)/shard_map/ppermute | solution.py:29
  108.0 7.3 %collective-permute-start.8 = (f32[32,768]{1,0:T(8,128)S(1)}, f32[32,768]{1,0:T(8,128)S(1)}, u32[]{:S(2)}, u32[]{:S(2)}) collective-permute-start(f32[32,768]{1,0:T(8,128)S(1)} %add.191), channel_id=1, source_target_pairs={{0,58},{2,60},{4,62},{6,0},{8,2},{10,4},{12,6},{14,8},{16,10},{18,... | collective-permute-start | bytes 294920 | tf_op jit(solution)/shard_map/ppermute | solution.py:29
  117.2 4.0 %collective-permute-done.8 = f32[32,768]{1,0:T(8,128)S(1)} collective-permute-done((f32[32,768]{1,0:T(8,128)S(1)}, f32[32,768]{1,0:T(8,128)S(1)}, u32[]{:S(2)}, u32[]{:S(2)}) %collective-permute-start.8) | collective-permute-done | bytes 98336 | tf_op jit(solution)/shard_map/ppermute | solution.py:29
  121.2 7.1 %collective-permute-start.10 = (f32[32,768]{1,0:T(8,128)S(1)}, f32[32,768]{1,0:T(8,128)S(1)}, u32[]{:S(2)}, u32[]{:S(2)}) collective-permute-start(f32[32,768]{1,0:T(8,128)S(1)} %add.193), channel_id=1, source_target_pairs={{0,58},{2,60},{4,62},{6,0},{8,2},{10,4},{12,6},{14,8},{16,10},{18,... | collective-permute-start | bytes 294920 | tf_op jit(solution)/shard_map/ppermute | solution.py:29
  130.3 3.4 %collective-permute-done.10 = f32[32,768]{1,0:T(8,128)S(1)} collective-permute-done((f32[32,768]{1,0:T(8,128)S(1)}, f32[32,768]{1,0:T(8,128)S(1)}, u32[]{:S(2)}, u32[]{:S(2)}) %collective-permute-start.10) | collective-permute-done | bytes 98336 | tf_op jit(solution)/shard_map/ppermute | solution.py:29
  133.7 5.1 %collective-permute-done.12 = f32[32,768]{1,0:T(8,128)S(1)} collective-permute-done((f32[32,768]{1,0:T(8,128)S(1)}, f32[32,768]{1,0:T(8,128)S(1)}, u32[]{:S(2)}, u32[]{:S(2)}) %collective-permute-start.12) | collective-permute-done | bytes 98336 | tf_op jit(solution)/shard_map/ppermute | solution.py:29
  141.4 6.4 %collective-permute-start.18 = (bf16[32,768]{1,0:T(8,128)(2,1)S(1)}, bf16[32,768]{1,0:T(8,128)(2,1)S(1)}, u32[]{:S(2)}, u32[]{:S(2)}) collective-permute-start(bf16[32,768]{1,0:T(8,128)(2,1)S(1)} %get-tuple-element.46), channel_id=1, source_target_pairs={{0,58},{2,60},{4,62},{6,0},{8,2},{10,4},{12,6},{14,8},{16,10},{18,... | collective-permute-start | bytes 147464 | tf_op jit(solution)/shard_map/ppermute | solution.py:29
  149.7 6.4 %collective-permute-start.19 = (bf16[32,768]{1,0:T(8,128)(2,1)S(1)}, bf16[32,768]{1,0:T(8,128)(2,1)S(1)}, u32[]{:S(2)}, u32[]{:S(2)}) collective-permute-start(bf16[32,768]{1,0:T(8,128)(2,1)S(1)} %collective-permute-done.18), channel_id=1, source_target_pairs={{0,58},{2,60},{4,62},{6,0},{8,2},{10,4},{12,6},{14,8},{16,10},{18,... | collective-permute-start | bytes 147464 | tf_op jit(solution)/shard_map/ppermute | solution.py:29
  158.0 6.4 %collective-permute-start.20 = (bf16[32,768]{1,0:T(8,128)(2,1)S(1)}, bf16[32,768]{1,0:T(8,128)(2,1)S(1)}, u32[]{:S(2)}, u32[]{:S(2)}) collective-permute-start(bf16[32,768]{1,0:T(8,128)(2,1)S(1)} %collective-permute-done.19), channel_id=1, source_target_pairs={{0,58},{2,60},{4,62},{6,0},{8,2},{10,4},{12,6},{14,8},{16,10},{18,... | collective-permute-start | bytes 147464 | tf_op jit(solution)/shard_map/ppermute | solution.py:29
  164.4 2.1 collective-permute-start.16
  166.6 6.2 %collective-permute-start.21 = (bf16[32,768]{1,0:T(8,128)(2,1)S(1)}, bf16[32,768]{1,0:T(8,128)(2,1)S(1)}, u32[]{:S(2)}, u32[]{:S(2)}) collective-permute-start(bf16[32,768]{1,0:T(8,128)(2,1)S(1)} %collective-permute-done.20), channel_id=1, source_target_pairs={{0,58},{2,60},{4,62},{6,0},{8,2},{10,4},{12,6},{14,8},{16,10},{18,... | collective-permute-start | bytes 147464 | tf_op jit(solution)/shard_map/ppermute | solution.py:29
  174.7 6.7 %collective-permute-start.22 = (bf16[32,768]{1,0:T(8,128)(2,1)S(1)}, bf16[32,768]{1,0:T(8,128)(2,1)S(1)}, u32[]{:S(2)}, u32[]{:S(2)}) collective-permute-start(bf16[32,768]{1,0:T(8,128)(2,1)S(1)} %collective-permute-done.21), channel_id=1, source_target_pairs={{0,58},{2,60},{4,62},{6,0},{8,2},{10,4},{12,6},{14,8},{16,10},{18,... | collective-permute-start | bytes 147464 | tf_op jit(solution)/shard_map/ppermute | solution.py:29
  181.5 2.0 collective-permute-done.22
  183.6 13.0 %collective-permute-start.23 = (bf16[10,32,768]{2,1,0:T(8,128)(2,1)S(1)}, bf16[10,32,768]{2,1,0:T(8,128)(2,1)S(1)}, u32[]{:S(2)}, u32[]{:S(2)}) collective-permute-start(bf16[10,32,768]{2,1,0:T(8,128)(2,1)S(1)} %slice.153), channel_id=1, source_target_pairs={{0,62},{2,0},{4,2},{6,4},{8,6},{10,8},{12,10},{14,12},{16,14},{18,... | collective-permute-start | bytes 1474568 | tf_op jit(solution)/shard_map/ppermute | solution.py:29
  198.5 6.1 %collective-permute-done.23 = bf16[10,32,768]{2,1,0:T(8,128)(2,1)S(1)} collective-permute-done((bf16[10,32,768]{2,1,0:T(8,128)(2,1)S(1)}, bf16[10,32,768]{2,1,0:T(8,128)(2,1)S(1)}, u32[]{:S(2)}, u32[]{:S(2)}) %collective-permute-start.23) | collective-permute-done | bytes 491552 | tf_op jit(solution)/shard_map/ppermute | solution.py:29
  205.4 5.3 %collective-permute-done.24 = bf16[11,32,768]{2,1,0:T(8,128)(2,1)S(1)} collective-permute-done((bf16[11,32,768]{2,1,0:T(8,128)(2,1)S(1)}, bf16[11,32,768]{2,1,0:T(8,128)(2,1)S(1)}, u32[]{:S(2)}, u32[]{:S(2)}) %collective-permute-start.24) | collective-permute-done | bytes 540704 | tf_op jit(solution)/shard_map/ppermute | solution.py:29
  212.4 5.6 %collective-permute-start.25 = (bf16[768,768]{1,0:T(8,128)(2,1)S(1)}, bf16[768,768]{1,0:T(8,128)(2,1)S(1)}, u32[]{:S(2)}, u32[]{:S(2)}) collective-permute-start(bf16[768,768]{1,0:T(8,128)(2,1)S(1)} %fusion.own_ref), channel_id=1, source_target_pairs={{0,1},{1,0},{2,3},{3,2},{4,5},{5,4},{6,7},{7,6},{8,9},{9,8},{10,11... | collective-permute-start | bytes 3538952 | tf_op jit(solution)/shard_map/ppermute | solution.py:33
  218.0 2.5 %collective-permute-done.25.other_ref = bf16[768,768]{1,0:T(8,128)(2,1)S(1)} collective-permute-done((bf16[768,768]{1,0:T(8,128)(2,1)S(1)}, bf16[768,768]{1,0:T(8,128)(2,1)S(1)}, u32[]{:S(2)}, u32[]{:S(2)}) %collective-permute-start.25) | collective-permute-done | bytes 1179680 | tf_op jit(solution)/shard_map/ppermute | solution.py:33
  221.4 5.6 %newton.1 = f32[32,768]{1,0:T(8,128)} custom-call(f32[32,768]{1,0:T(8,128)} %get-tuple-element.47.velocity_ref, bf16[768,768]{1,0:T(8,128)(2,1)} %copy-done.1, bf16[768,768]{1,0:T(8,128)(2,1)} %copy-done.2), custom_call_target="tpu_custom_call" | custom-call | tf_op jit(solution)/shard_map/newton/pallas_call | solution.py:228
  (69 shorter events, 27.3 us)
Async XLA Ops:
  4.8 17.2 %copy-start.4 = (bf16[1,1,16,24,768]{4,3,2,1,0:T(8,128)(2,1)S(1)}, bf16[1,1,16,24,768]{4,3,2,1,0:T(8,128)(2,1)}, u32[]{:S(2)}) copy-start(bf16[1,1,16,24,768]{4,3,2,1,0:T(8,128)(2,1)} %param.9) | copy-start | bytes 1769476
  4.8 19.5 %copy-start.6 = (s32[32]{0:T(128)S(1)}, s32[32]{0:T(128)}, u32[]{:S(2)}) copy-start(s32[32]{0:T(128)} %constant.34) | copy-start | bytes 388
  4.8 39.1 %all-to-all-start = ((bf16[32,24,1024]{2,1,0:T(8,128)(2,1)}), bf16[32,24,1024]{2,1,0:T(8,128)(2,1)S(1)}, u32[]{:S(2)}, u32[]{:S(2)}) async-start(bf16[32,24,1024]{2,1,0:T(8,128)(2,1)} %route.1), calls=%async_computation | async-start | bytes 3145728 | tf_op jit(solution)/shard_map/all_to_all | solution.py:190
  22.0 3.9 %collective-permute-start = (bf16[16,24,768]{2,1,0:T(8,128)(2,1)S(1)}, bf16[16,24,768]{2,1,0:T(8,128)(2,1)S(1)}, u32[]{:S(2)}, u32[]{:S(2)}) collective-permute-start(bf16[16,24,768]{2,1,0:T(8,128)(2,1)S(1)} %bitcast.83), channel_id=1, source_target_pairs={{0,1},{1,0},{2,3},{3,2},{4,5},{5,4},{6,7},{7,6},{8,9},{9,8},{10,11... | collective-permute-start | bytes 1769480 | tf_op jit(solution)/shard_map/ppermute | solution.py:33
  49.7 23.5 %copy-start.3 = (f32[11,32,768]{2,1,0:T(8,128)S(1)}, f32[11,32,768]{2,1,0:T(8,128)}, u32[]{:S(2)}) copy-start(f32[11,32,768]{2,1,0:T(8,128)} %get-tuple-element.24) | copy-start | bytes 3244036
  49.7 22.4 %collective-permute-start.1 = (bf16[11,32,768]{2,1,0:T(8,128)(2,1)}, bf16[11,32,768]{2,1,0:T(8,128)(2,1)S(1)}, u32[]{:S(2)}, u32[]{:S(2)}) collective-permute-start(bf16[11,32,768]{2,1,0:T(8,128)(2,1)} %get-tuple-element.25), channel_id=1, source_target_pairs={{0,2},{2,4},{4,6},{6,8},{8,10},{10,12},{12,14},{14,16},{16,18},{18... | collective-permute-start | bytes 1622024 | tf_op jit(solution)/shard_map/ppermute | solution.py:29
  51.8 20.3 %collective-permute-start.2 = (bf16[10,32,768]{2,1,0:T(8,128)(2,1)}, bf16[10,32,768]{2,1,0:T(8,128)(2,1)S(1)}, u32[]{:S(2)}, u32[]{:S(2)}) collective-permute-start(bf16[10,32,768]{2,1,0:T(8,128)(2,1)} %get-tuple-element.26), channel_id=1, source_target_pairs={{0,62},{2,0},{4,2},{6,4},{8,6},{10,8},{12,10},{14,12},{16,14},{18,... | collective-permute-start | bytes 1474568 | tf_op jit(solution)/shard_map/ppermute | solution.py:29
  73.3 65.4 %copy-start.5 = (f32[1,32,768]{2,1,0:T(8,128)S(1)}, f32[1,32,768]{2,1,0:T(8,128)}, u32[]{:S(2)}) copy-start(f32[1,32,768]{2,1,0:T(8,128)} %param.10) | copy-start | bytes 294916
  73.3 7.7 %collective-permute-start.3 = (f32[32,768]{1,0:T(8,128)S(1)}, f32[32,768]{1,0:T(8,128)S(1)}, u32[]{:S(2)}, u32[]{:S(2)}) collective-permute-start(f32[32,768]{1,0:T(8,128)S(1)} %get-tuple-element.32), channel_id=1, source_target_pairs={{0,58},{2,60},{4,62},{6,0},{8,2},{10,4},{12,6},{14,8},{16,10},{18,... | collective-permute-start | bytes 294920 | tf_op jit(solution)/shard_map/ppermute | solution.py:29
  78.8 10.5 %collective-permute-start.5 = (f32[32,768]{1,0:T(8,128)S(1)}, f32[32,768]{1,0:T(8,128)S(1)}, u32[]{:S(2)}, u32[]{:S(2)}) collective-permute-start(f32[32,768]{1,0:T(8,128)S(1)} %get-tuple-element.33), channel_id=1, source_target_pairs={{0,6},{2,8},{4,10},{6,12},{8,14},{10,16},{12,18},{14,20},{16,22},{... | collective-permute-start | bytes 294920 | tf_op jit(solution)/shard_map/ppermute | solution.py:29
  81.0 10.3 %collective-permute-start.4 = (f32[32,768]{1,0:T(8,128)S(1)}, f32[32,768]{1,0:T(8,128)S(1)}, u32[]{:S(2)}, u32[]{:S(2)}) collective-permute-start(f32[32,768]{1,0:T(8,128)S(1)} %add.187), channel_id=1, source_target_pairs={{0,58},{2,60},{4,62},{6,0},{8,2},{10,4},{12,6},{14,8},{16,10},{18,... | collective-permute-start | bytes 294920 | tf_op jit(solution)/shard_map/ppermute | solution.py:29
  89.4 12.1 %collective-permute-start.7 = (f32[32,768]{1,0:T(8,128)S(1)}, f32[32,768]{1,0:T(8,128)S(1)}, u32[]{:S(2)}, u32[]{:S(2)}) collective-permute-start(f32[32,768]{1,0:T(8,128)S(1)} %add.188), channel_id=1, source_target_pairs={{0,6},{2,8},{4,10},{6,12},{8,14},{10,16},{12,18},{14,20},{16,22},{... | collective-permute-start | bytes 294920 | tf_op jit(solution)/shard_map/ppermute | solution.py:29
  91.3 16.6 %collective-permute-start.6 = (f32[32,768]{1,0:T(8,128)S(1)}, f32[32,768]{1,0:T(8,128)S(1)}, u32[]{:S(2)}, u32[]{:S(2)}) collective-permute-start(f32[32,768]{1,0:T(8,128)S(1)} %add.189), channel_id=1, source_target_pairs={{0,58},{2,60},{4,62},{6,0},{8,2},{10,4},{12,6},{14,8},{16,10},{18,... | collective-permute-start | bytes 294920 | tf_op jit(solution)/shard_map/ppermute | solution.py:29
  101.5 13.7 %collective-permute-start.9 = (f32[32,768]{1,0:T(8,128)S(1)}, f32[32,768]{1,0:T(8,128)S(1)}, u32[]{:S(2)}, u32[]{:S(2)}) collective-permute-start(f32[32,768]{1,0:T(8,128)S(1)} %add.190), channel_id=1, source_target_pairs={{0,6},{2,8},{4,10},{6,12},{8,14},{10,16},{12,18},{14,20},{16,22},{... | collective-permute-start | bytes 294920 | tf_op jit(solution)/shard_map/ppermute | solution.py:29
  108.0 13.2 %collective-permute-start.8 = (f32[32,768]{1,0:T(8,128)S(1)}, f32[32,768]{1,0:T(8,128)S(1)}, u32[]{:S(2)}, u32[]{:S(2)}) collective-permute-start(f32[32,768]{1,0:T(8,128)S(1)} %add.191), channel_id=1, source_target_pairs={{0,58},{2,60},{4,62},{6,0},{8,2},{10,4},{12,6},{14,8},{16,10},{18,... | collective-permute-start | bytes 294920 | tf_op jit(solution)/shard_map/ppermute | solution.py:29
  115.3 13.1 %collective-permute-start.11 = (f32[32,768]{1,0:T(8,128)S(1)}, f32[32,768]{1,0:T(8,128)S(1)}, u32[]{:S(2)}, u32[]{:S(2)}) collective-permute-start(f32[32,768]{1,0:T(8,128)S(1)} %add.192), channel_id=1, source_target_pairs={{0,6},{2,8},{4,10},{6,12},{8,14},{10,16},{12,18},{14,20},{16,22},{... | collective-permute-start | bytes 294920 | tf_op jit(solution)/shard_map/ppermute | solution.py:29
  121.2 12.5 %collective-permute-start.10 = (f32[32,768]{1,0:T(8,128)S(1)}, f32[32,768]{1,0:T(8,128)S(1)}, u32[]{:S(2)}, u32[]{:S(2)}) collective-permute-start(f32[32,768]{1,0:T(8,128)S(1)} %add.193), channel_id=1, source_target_pairs={{0,58},{2,60},{4,62},{6,0},{8,2},{10,4},{12,6},{14,8},{16,10},{18,... | collective-permute-start | bytes 294920 | tf_op jit(solution)/shard_map/ppermute | solution.py:29
  128.4 10.4 %collective-permute-start.12 = (f32[32,768]{1,0:T(8,128)S(1)}, f32[32,768]{1,0:T(8,128)S(1)}, u32[]{:S(2)}, u32[]{:S(2)}) collective-permute-start(f32[32,768]{1,0:T(8,128)S(1)} %add.195), channel_id=1, source_target_pairs={{0,6},{2,8},{4,10},{6,12},{8,14},{10,16},{12,18},{14,20},{16,22},{... | collective-permute-start | bytes 294920 | tf_op jit(solution)/shard_map/ppermute | solution.py:29
  139.5 8.3 %collective-permute-start.13 = (bf16[32,768]{1,0:T(8,128)(2,1)S(1)}, bf16[32,768]{1,0:T(8,128)(2,1)S(1)}, u32[]{:S(2)}, u32[]{:S(2)}) collective-permute-start(bf16[32,768]{1,0:T(8,128)(2,1)S(1)} %get-tuple-element.46), channel_id=1, source_target_pairs={{0,6},{2,8},{4,10},{6,12},{8,14},{10,16},{12,18},{14,20},{16,22},{... | collective-permute-start | bytes 147464 | tf_op jit(solution)/shard_map/ppermute | solution.py:29
  141.4 8.3 %collective-permute-start.18 = (bf16[32,768]{1,0:T(8,128)(2,1)S(1)}, bf16[32,768]{1,0:T(8,128)(2,1)S(1)}, u32[]{:S(2)}, u32[]{:S(2)}) collective-permute-start(bf16[32,768]{1,0:T(8,128)(2,1)S(1)} %get-tuple-element.46), channel_id=1, source_target_pairs={{0,58},{2,60},{4,62},{6,0},{8,2},{10,4},{12,6},{14,8},{16,10},{18,... | collective-permute-start | bytes 147464 | tf_op jit(solution)/shard_map/ppermute | solution.py:29
  147.8 8.3 %collective-permute-start.14 = (bf16[32,768]{1,0:T(8,128)(2,1)S(1)}, bf16[32,768]{1,0:T(8,128)(2,1)S(1)}, u32[]{:S(2)}, u32[]{:S(2)}) collective-permute-start(bf16[32,768]{1,0:T(8,128)(2,1)S(1)} %collective-permute-done.13), channel_id=1, source_target_pairs={{0,6},{2,8},{4,10},{6,12},{8,14},{10,16},{12,18},{14,20},{16,22},{... | collective-permute-start | bytes 147464 | tf_op jit(solution)/shard_map/ppermute | solution.py:29
  149.7 8.3 %collective-permute-start.19 = (bf16[32,768]{1,0:T(8,128)(2,1)S(1)}, bf16[32,768]{1,0:T(8,128)(2,1)S(1)}, u32[]{:S(2)}, u32[]{:S(2)}) collective-permute-start(bf16[32,768]{1,0:T(8,128)(2,1)S(1)} %collective-permute-done.18), channel_id=1, source_target_pairs={{0,58},{2,60},{4,62},{6,0},{8,2},{10,4},{12,6},{14,8},{16,10},{18,... | collective-permute-start | bytes 147464 | tf_op jit(solution)/shard_map/ppermute | solution.py:29
  156.1 8.3 %collective-permute-start.15 = (bf16[32,768]{1,0:T(8,128)(2,1)S(1)}, bf16[32,768]{1,0:T(8,128)(2,1)S(1)}, u32[]{:S(2)}, u32[]{:S(2)}) collective-permute-start(bf16[32,768]{1,0:T(8,128)(2,1)S(1)} %collective-permute-done.14), channel_id=1, source_target_pairs={{0,6},{2,8},{4,10},{6,12},{8,14},{10,16},{12,18},{14,20},{16,22},{... | collective-permute-start | bytes 147464 | tf_op jit(solution)/shard_map/ppermute | solution.py:29
  158.0 8.5 %collective-permute-start.20 = (bf16[32,768]{1,0:T(8,128)(2,1)S(1)}, bf16[32,768]{1,0:T(8,128)(2,1)S(1)}, u32[]{:S(2)}, u32[]{:S(2)}) collective-permute-start(bf16[32,768]{1,0:T(8,128)(2,1)S(1)} %collective-permute-done.19), channel_id=1, source_target_pairs={{0,58},{2,60},{4,62},{6,0},{8,2},{10,4},{12,6},{14,8},{16,10},{18,... | collective-permute-start | bytes 147464 | tf_op jit(solution)/shard_map/ppermute | solution.py:29
  164.4 8.3 %collective-permute-start.16 = (bf16[32,768]{1,0:T(8,128)(2,1)S(1)}, bf16[32,768]{1,0:T(8,128)(2,1)S(1)}, u32[]{:S(2)}, u32[]{:S(2)}) collective-permute-start(bf16[32,768]{1,0:T(8,128)(2,1)S(1)} %collective-permute-done.15), channel_id=1, source_target_pairs={{0,6},{2,8},{4,10},{6,12},{8,14},{10,16},{12,18},{14,20},{16,22},{... | collective-permute-start | bytes 147464 | tf_op jit(solution)/shard_map/ppermute | solution.py:29
  166.6 8.1 %collective-permute-start.21 = (bf16[32,768]{1,0:T(8,128)(2,1)S(1)}, bf16[32,768]{1,0:T(8,128)(2,1)S(1)}, u32[]{:S(2)}, u32[]{:S(2)}) collective-permute-start(bf16[32,768]{1,0:T(8,128)(2,1)S(1)} %collective-permute-done.20), channel_id=1, source_target_pairs={{0,58},{2,60},{4,62},{6,0},{8,2},{10,4},{12,6},{14,8},{16,10},{18,... | collective-permute-start | bytes 147464 | tf_op jit(solution)/shard_map/ppermute | solution.py:29
  172.8 8.6 %collective-permute-start.17 = (bf16[32,768]{1,0:T(8,128)(2,1)S(1)}, bf16[32,768]{1,0:T(8,128)(2,1)S(1)}, u32[]{:S(2)}, u32[]{:S(2)}) collective-permute-start(bf16[32,768]{1,0:T(8,128)(2,1)S(1)} %collective-permute-done.16), channel_id=1, source_target_pairs={{0,6},{2,8},{4,10},{6,12},{8,14},{10,16},{12,18},{14,20},{16,22},{... | collective-permute-start | bytes 147464 | tf_op jit(solution)/shard_map/ppermute | solution.py:29
  174.7 8.8 %collective-permute-start.22 = (bf16[32,768]{1,0:T(8,128)(2,1)S(1)}, bf16[32,768]{1,0:T(8,128)(2,1)S(1)}, u32[]{:S(2)}, u32[]{:S(2)}) collective-permute-start(bf16[32,768]{1,0:T(8,128)(2,1)S(1)} %collective-permute-done.21), channel_id=1, source_target_pairs={{0,58},{2,60},{4,62},{6,0},{8,2},{10,4},{12,6},{14,8},{16,10},{18,... | collective-permute-start | bytes 147464 | tf_op jit(solution)/shard_map/ppermute | solution.py:29
  183.6 21.0 %collective-permute-start.23 = (bf16[10,32,768]{2,1,0:T(8,128)(2,1)S(1)}, bf16[10,32,768]{2,1,0:T(8,128)(2,1)S(1)}, u32[]{:S(2)}, u32[]{:S(2)}) collective-permute-start(bf16[10,32,768]{2,1,0:T(8,128)(2,1)S(1)} %slice.153), channel_id=1, source_target_pairs={{0,62},{2,0},{4,2},{6,4},{8,6},{10,8},{12,10},{14,12},{16,14},{18,... | collective-permute-start | bytes 1474568 | tf_op jit(solution)/shard_map/ppermute | solution.py:29
  196.6 14.1 %collective-permute-start.24 = (bf16[11,32,768]{2,1,0:T(8,128)(2,1)S(1)}, bf16[11,32,768]{2,1,0:T(8,128)(2,1)S(1)}, u32[]{:S(2)}, u32[]{:S(2)}) collective-permute-start(bf16[11,32,768]{2,1,0:T(8,128)(2,1)S(1)} %bitcast_dynamic-update-slice_fusion), channel_id=1, source_target_pairs={{0,2},{2,4},{4,6},{6,8},{8,10},{10,12},{12,14},{14,16},{16,18},{18... | collective-permute-start | bytes 1622024 | tf_op jit(solution)/shard_map/ppermute | solution.py:29
  212.4 8.0 %copy-start.1 = (bf16[768,768]{1,0:T(8,128)(2,1)}, bf16[768,768]{1,0:T(8,128)(2,1)S(1)}, u32[]{:S(2)}) copy-start(bf16[768,768]{1,0:T(8,128)(2,1)S(1)} %fusion.own_ref) | copy-start | bytes 3538948
  212.4 8.0 %collective-permute-start.25 = (bf16[768,768]{1,0:T(8,128)(2,1)S(1)}, bf16[768,768]{1,0:T(8,128)(2,1)S(1)}, u32[]{:S(2)}, u32[]{:S(2)}) collective-permute-start(bf16[768,768]{1,0:T(8,128)(2,1)S(1)} %fusion.own_ref), channel_id=1, source_target_pairs={{0,1},{1,0},{2,3},{3,2},{4,5},{5,4},{6,7},{7,6},{8,9},{9,8},{10,11... | collective-permute-start | bytes 3538952 | tf_op jit(solution)/shard_map/ppermute | solution.py:33
  (2 other events, 2.2 us)

commit v3 on v2

--- a/solution.py
+++ b/solution.py
@@ -15,15 +15,18 @@
 EPSILON = 1e-07
 
 STRIDE = 3
-REACH = 5
-FAR = range(-REACH, REACH + 1)
-UP = tuple(a for a in FAR if a < REACH)
-DOWN = tuple(FAR)
+BASE = (0, 3, -3)
+ABOVE = (1, 4, -2)
+BELOW = (-1, 2, -4)
+STEPS = BASE + ABOVE + BELOW + (-5, 5)
+UP = STEPS[:-1]
+DOWN = STEPS
 OFFSETS = (
     tuple(STRIDE * a + 1 for a in UP)
     + tuple(STRIDE * a - 1 for a in DOWN)
-    + tuple(STRIDE * a for a in FAR)
+    + tuple(STRIDE * a for a in STEPS)
 )
+
 
 def shifted(x, by, ring):
     return lax.ppermute(x, "z", [(i, (i + by) % ring) for i in range(ring)])
@@ -126,30 +129,26 @@
     out_ref[...] = final * jnp.sqrt(jnp.float32(D))
 
 
-def after(x, earlier):
-    return lax.optimization_barrier((x, earlier))[0]
-
-
 def reduce_over_ring(up, down, middle, ring):
-    f32 = jnp.float32
+    f32, bf16 = jnp.float32, jnp.bfloat16
     up = shifted(up, -1, ring)
     down = shifted(down, 1, ring)
-    sums = {}
-    for n, a in enumerate(FAR):
-        sums[a] = middle[n] + down[DOWN.index(a)].astype(f32)
-        if a in UP:
-            sums[a] = sums[a] + up[UP.index(a)].astype(f32)
+    sums = middle + down.astype(f32)
+    sums = jnp.concatenate([sums[:-1] + up.astype(f32), sums[-1:]])
     sums = lax.optimization_barrier(sums)
-    got = {}
-    last = None
-    for k in range(REACH, 0, -1):
-        for side in (1, -1):
-            total = sums[side * k]
-            if side in got:
-                total = total + after(got[side], last)
-            last = total
-            got[side] = shifted(total, -side * STRIDE, ring)
-    return sums[0] + got[1] + got[-1]
+    base, above, below = sums[0:3], sums[3:6], sums[6:9]
+    up = shifted(sums[10].astype(bf16), -STRIDE, ring).astype(f32)
+    down = shifted(sums[9].astype(bf16), STRIDE, ring).astype(f32)
+    above = jnp.stack([above[0], above[1] + up, above[2]]).astype(bf16)
+    below = jnp.stack([below[0], below[1], below[2] + down]).astype(bf16)
+    above, below = lax.optimization_barrier((above, below))
+    up = shifted(above, -STRIDE, ring)
+    down = shifted(below, STRIDE, ring)
+    base = base + up.astype(f32) + down.astype(f32)
+    far = lax.optimization_barrier((base[0], base[1].astype(bf16), base[2].astype(bf16)))
+    up = shifted(far[1], -3 * STRIDE, ring)
+    down = shifted(far[2], 3 * STRIDE, ring)
+    return far[0] + up.astype(f32) + down.astype(f32)
 
 
 def gram_of(blocks):
@@ -160,12 +159,13 @@
 
 
 def gram_over_ring(own, ring):
-    held = {0: own}
-    for k in range(1, REACH + 1):
-        for side in (1, -1):
-            held[side * k] = shifted(held[side * (k - 1)], -side * STRIDE, ring)
-    rows = lax.optimization_barrier(jnp.stack([held[a] for a in FAR]))
-    up = shifted(rows[: len(UP)], -1, ring)
+    base = jnp.stack([own, shifted(own, -3 * STRIDE, ring), shifted(own, 3 * STRIDE, ring)])
+    above = shifted(base, -STRIDE, ring)
+    below = shifted(base, STRIDE, ring)
+    up = shifted(above[1:2], -STRIDE, ring)
+    down = shifted(below[2:3], STRIDE, ring)
+    rows = lax.optimization_barrier(jnp.concatenate([base, above, below, down, up]))
+    up = shifted(rows[:-1], -1, ring)
     down = shifted(rows, 1, ring)
     return gram_of(rows) + gram_of(up) + gram_of(down)
 
@@ -205,7 +205,7 @@
         out_shape=(
             jax.ShapeDtypeStruct((len(UP), d_local, units), bf16),
             jax.ShapeDtypeStruct((len(DOWN), d_local, units), bf16),
-            jax.ShapeDtypeStruct((len(FAR), d_local, units), f32),
+            jax.ShapeDtypeStruct((len(STEPS), d_local, units), f32),
         ),
         in_specs=[
             pl.BlockSpec(memory_space=pltpu.SMEM),

time: 228 us -> 214 us (0.939)
  the two profiles are of different devices: /device:TPU:9 before, /device:TPU:1 now
where the time goes in v3:
time: 214 us; the launch traced here: 210 us
  starting transfers between devices  118 us (55%)
  waiting for transfers between devices  67.4 us (31%)
  Pallas kernels  14.4 us (7%)
  other arithmetic  3.76 us (2%)
  local copies, waits for them, and re-layouts  3.48 us (2%)
  matrix products  2.48 us (1%)
    ppermute x16, starting transfers between devices, shifted(): return lax.ppermute(x, 'z', [(i, (i + by) % ring) for i in range(ring)])  80.9 us
    ppermute x16, waiting for transfers between devices, shifted(): return lax.ppermute(x, 'z', [(i, (i + by) % ring) for i in range(ring)])  47.4 us
    ppermute x2, starting transfers between devices, swapped(): return lax.ppermute(x, 'core', [(0, 1), (1, 0)])  19 us
    all_to_all x1, starting transfers between devices, local(): lax.all_to_all(outgoing, ('expert', 'core'), split_axis=0, concat_axis=0,...  17.9 us
    all_to_all x1, waiting for transfers between devices, local(): lax.all_to_all(outgoing, ('expert', 'core'), split_axis=0, concat_axis=0,...  17.1 us
    pallas_call x1, Pallas kernels, local(): pl.pallas_call(newton_kernel, out_shape=jax.ShapeDtypeStruct((d_local, un...  5.63 us
    pallas_call x1, Pallas kernels, local(): pl.pallas_call(partial_kernel, out_shape=(jax.ShapeDtypeStruct((len(UP),...  4.58 us
  transfers between devices with their start and end apart: 19, of which 15 were waited for; matrix products, arithmetic and copies ran while one was open for 3% of the time, Pallas kernels for 0%

profile of v3, /device:TPU:1, one launch (start us, length us, event | category | flops | bytes accessed | tf_op | source)
XLA Modules:
  0.0 210.4 jit_solution(16815590754247152460)
XLA Ops:
  0.6 4.2 %route.1 = bf16[32,24,1024]{2,1,0:T(8,128)(2,1)} custom-call(s32[1,256]{1,0:T(1,128)} %bitcast.80, f32[1,256]{1,0:T(1,128)} %bitcast.81, bf16[256,2048]{1,0:T(8,128)(2,1)} %refs_2_.1), custom_call_target="tpu_custom_call" | custom-call | tf_op jit(solution)/shard_map/route/pallas_call | solution.py:185
  4.8 17.9 %all-to-all-start = ((bf16[32,24,1024]{2,1,0:T(8,128)(2,1)}), bf16[32,24,1024]{2,1,0:T(8,128)(2,1)S(1)}, u32[]{:S(2)}, u32[]{:S(2)}) async-start(bf16[32,24,1024]{2,1,0:T(8,128)(2,1)} %route.1), calls=%async_computation | async-start | bytes 3145728 | tf_op jit(solution)/shard_map/all_to_all | solution.py:190
  22.7 2.3 %collective-permute-start = (bf16[16,24,768]{2,1,0:T(8,128)(2,1)S(1)}, bf16[16,24,768]{2,1,0:T(8,128)(2,1)S(1)}, u32[]{:S(2)}, u32[]{:S(2)}) collective-permute-start(bf16[16,24,768]{2,1,0:T(8,128)(2,1)S(1)} %bitcast.75), channel_id=1, source_target_pairs={{0,1},{1,0},{2,3},{3,2},{4,5},{5,4},{6,7},{7,6},{8,9},{9,8},{10,11... | collective-permute-start | bytes 1769480 | tf_op jit(solution)/shard_map/ppermute | solution.py:36
  27.9 17.1 %all-to-all-done = bf16[32,24,1024]{2,1,0:T(8,128)(2,1)S(1)} async-done(((bf16[32,24,1024]{2,1,0:T(8,128)(2,1)}), bf16[32,24,1024]{2,1,0:T(8,128)(2,1)S(1)}, u32[]{:S(2)}, u32[]{:S(2)}) %all-to-all-start) | async-done | bytes 1572896 | tf_op jit(solution)/shard_map/all_to_all | solution.py:190
  46.2 4.6 %partial.1 = (bf16[10,32,768]{2,1,0:T(8,128)(2,1)}, bf16[11,32,768]{2,1,0:T(8,128)(2,1)}, f32[11,32,768]{2,1,0:T(8,128)}) custom-call(s32[32]{0:T(128)} %and_select_fusion.chunk_ref, bf16[768,1024]{1,0:T(8,128)(2,1)} %bitcast.73, bf16[768,768]{1,0:T(8,128)(2,1)} %bitcast.74), custom_call_target="tpu_custom_call" | custom-call | tf_op jit(solution)/shard_map/partial/pallas_call | solution.py:203
  50.8 1.9 collective-permute-start.1
  52.7 9.1 %collective-permute-start.2 = (bf16[10,32,768]{2,1,0:T(8,128)(2,1)}, bf16[10,32,768]{2,1,0:T(8,128)(2,1)S(1)}, u32[]{:S(2)}, u32[]{:S(2)}) collective-permute-start(bf16[10,32,768]{2,1,0:T(8,128)(2,1)} %get-tuple-element.12), channel_id=1, source_target_pairs={{0,62},{2,0},{4,2},{6,4},{8,6},{10,8},{12,10},{14,12},{16,14},{18,... | collective-permute-start | bytes 1474568 | tf_op jit(solution)/shard_map/ppermute | solution.py:32
  61.8 9.0 %collective-permute-done.1 = bf16[11,32,768]{2,1,0:T(8,128)(2,1)S(1)} collective-permute-done((bf16[11,32,768]{2,1,0:T(8,128)(2,1)}, bf16[11,32,768]{2,1,0:T(8,128)(2,1)S(1)}, u32[]{:S(2)}, u32[]{:S(2)}) %collective-permute-start.1) | collective-permute-done | bytes 540704 | tf_op jit(solution)/shard_map/ppermute | solution.py:32
  72.4 1.9 collective-permute-start.4
  74.4 6.4 %collective-permute-start.3 = (bf16[32,768]{1,0:T(8,128)(2,1)S(1)}, bf16[32,768]{1,0:T(8,128)(2,1)S(1)}, u32[]{:S(2)}, u32[]{:S(2)}) collective-permute-start(bf16[32,768]{1,0:T(8,128)(2,1)S(1)} %get-tuple-element.29), channel_id=1, source_target_pairs={{0,58},{2,60},{4,62},{6,0},{8,2},{10,4},{12,6},{14,8},{16,10},{18,... | collective-permute-start | bytes 147464 | tf_op jit(solution)/shard_map/ppermute | solution.py:32
  82.0 6.8 %collective-permute-start.5 = (bf16[3,32,768]{2,1,0:T(8,128)(2,1)S(1)}, bf16[3,32,768]{2,1,0:T(8,128)(2,1)S(1)}, u32[]{:S(2)}, u32[]{:S(2)}) collective-permute-start(bf16[3,32,768]{2,1,0:T(8,128)(2,1)S(1)} %get-tuple-element.13), channel_id=1, source_target_pairs={{0,58},{2,60},{4,62},{6,0},{8,2},{10,4},{12,6},{14,8},{16,10},{18,... | collective-permute-start | bytes 442376 | tf_op jit(solution)/shard_map/ppermute | solution.py:32
  88.8 1.9 collective-permute-start.6
  90.7 2.2 %collective-permute-done.5 = bf16[3,32,768]{2,1,0:T(8,128)(2,1)S(1)} collective-permute-done((bf16[3,32,768]{2,1,0:T(8,128)(2,1)S(1)}, bf16[3,32,768]{2,1,0:T(8,128)(2,1)S(1)}, u32[]{:S(2)}, u32[]{:S(2)}) %collective-permute-start.5) | collective-permute-done | bytes 147488 | tf_op jit(solution)/shard_map/ppermute | solution.py:32
  92.9 7.5 %collective-permute-done.6 = bf16[3,32,768]{2,1,0:T(8,128)(2,1)S(1)} collective-permute-done((bf16[3,32,768]{2,1,0:T(8,128)(2,1)S(1)}, bf16[3,32,768]{2,1,0:T(8,128)(2,1)S(1)}, u32[]{:S(2)}, u32[]{:S(2)}) %collective-permute-start.6) | collective-permute-done | bytes 147488 | tf_op jit(solution)/shard_map/ppermute | solution.py:32
  100.5 5.0 %collective-permute-start.7 = (bf16[32,768]{1,0:T(8,128)(2,1)S(1)}, bf16[32,768]{1,0:T(8,128)(2,1)S(1)}, u32[]{:S(2)}, u32[]{:S(2)}) collective-permute-start(bf16[32,768]{1,0:T(8,128)(2,1)S(1)} %get-tuple-element.16), channel_id=1, source_target_pairs={{0,46},{2,48},{4,50},{6,52},{8,54},{10,56},{12,58},{14,60},{16,62}... | collective-permute-start | bytes 147464 | tf_op jit(solution)/shard_map/ppermute | solution.py:32
  105.5 9.9 %collective-permute-start.8 = (bf16[32,768]{1,0:T(8,128)(2,1)S(1)}, bf16[32,768]{1,0:T(8,128)(2,1)S(1)}, u32[]{:S(2)}, u32[]{:S(2)}) collective-permute-start(bf16[32,768]{1,0:T(8,128)(2,1)S(1)} %get-tuple-element.17), channel_id=1, source_target_pairs={{0,18},{2,20},{4,22},{6,24},{8,26},{10,28},{12,30},{14,32},{16,34}... | collective-permute-start | bytes 147464 | tf_op jit(solution)/shard_map/ppermute | solution.py:32
  116.0 5.1 %collective-permute-done.8 = bf16[32,768]{1,0:T(8,128)(2,1)S(1)} collective-permute-done((bf16[32,768]{1,0:T(8,128)(2,1)S(1)}, bf16[32,768]{1,0:T(8,128)(2,1)S(1)}, u32[]{:S(2)}, u32[]{:S(2)}) %collective-permute-start.8) | collective-permute-done | bytes 49184 | tf_op jit(solution)/shard_map/ppermute | solution.py:32
  121.8 9.3 %collective-permute-start.10 = (bf16[32,768]{1,0:T(8,128)(2,1)S(1)}, bf16[32,768]{1,0:T(8,128)(2,1)S(1)}, u32[]{:S(2)}, u32[]{:S(2)}) collective-permute-start(bf16[32,768]{1,0:T(8,128)(2,1)S(1)} %get-tuple-element.19), channel_id=1, source_target_pairs={{0,18},{2,20},{4,22},{6,24},{8,26},{10,28},{12,30},{14,32},{16,34}... | collective-permute-start | bytes 147464 | tf_op jit(solution)/shard_map/ppermute | solution.py:32
  131.1 6.8 %collective-permute-start.9 = (bf16[32,768]{1,0:T(8,128)(2,1)S(1)}, bf16[32,768]{1,0:T(8,128)(2,1)S(1)}, u32[]{:S(2)}, u32[]{:S(2)}) collective-permute-start(bf16[32,768]{1,0:T(8,128)(2,1)S(1)} %get-tuple-element.19), channel_id=1, source_target_pairs={{0,46},{2,48},{4,50},{6,52},{8,54},{10,56},{12,58},{14,60},{16,62}... | collective-permute-start | bytes 147464 | tf_op jit(solution)/shard_map/ppermute | solution.py:32
  137.9 9.0 %collective-permute-done.9 = bf16[32,768]{1,0:T(8,128)(2,1)S(1)} collective-permute-done((bf16[32,768]{1,0:T(8,128)(2,1)S(1)}, bf16[32,768]{1,0:T(8,128)(2,1)S(1)}, u32[]{:S(2)}, u32[]{:S(2)}) %collective-permute-start.9) | collective-permute-done | bytes 49184 | tf_op jit(solution)/shard_map/ppermute | solution.py:32
  147.0 1.9 collective-permute-start.12
  148.9 6.4 %collective-permute-start.11 = (bf16[3,32,768]{2,1,0:T(8,128)(2,1)S(1)}, bf16[3,32,768]{2,1,0:T(8,128)(2,1)S(1)}, u32[]{:S(2)}, u32[]{:S(2)}) collective-permute-start(bf16[3,32,768]{2,1,0:T(8,128)(2,1)S(1)} %pad_maximum_fusion.4), channel_id=1, source_target_pairs={{0,58},{2,60},{4,62},{6,0},{8,2},{10,4},{12,6},{14,8},{16,10},{18,... | collective-permute-start | bytes 442376 | tf_op jit(solution)/shard_map/ppermute | solution.py:32
  155.3 2.3 %collective-permute-done.12 = bf16[3,32,768]{2,1,0:T(8,128)(2,1)S(1)} collective-permute-done((bf16[3,32,768]{2,1,0:T(8,128)(2,1)S(1)}, bf16[3,32,768]{2,1,0:T(8,128)(2,1)S(1)}, u32[]{:S(2)}, u32[]{:S(2)}) %collective-permute-start.12) | collective-permute-done | bytes 147488 | tf_op jit(solution)/shard_map/ppermute | solution.py:32
  157.6 1.9 collective-permute-start.13
  159.5 6.5 %collective-permute-start.14 = (bf16[1,32,768]{2,1,0:T(8,128)(2,1)S(1)}, bf16[1,32,768]{2,1,0:T(8,128)(2,1)S(1)}, u32[]{:S(2)}, u32[]{:S(2)}) collective-permute-start(bf16[1,32,768]{2,1,0:T(8,128)(2,1)S(1)} %slice.95), channel_id=1, source_target_pairs={{0,58},{2,60},{4,62},{6,0},{8,2},{10,4},{12,6},{14,8},{16,10},{18,... | collective-permute-start | bytes 147464 | tf_op jit(solution)/shard_map/ppermute | solution.py:32
  166.1 3.7 %collective-permute-done.13 = bf16[1,32,768]{2,1,0:T(8,128)(2,1)S(1)} collective-permute-done((bf16[1,32,768]{2,1,0:T(8,128)(2,1)S(1)}, bf16[1,32,768]{2,1,0:T(8,128)(2,1)S(1)}, u32[]{:S(2)}, u32[]{:S(2)}) %collective-permute-start.13) | collective-permute-done | bytes 49184 | tf_op jit(solution)/shard_map/ppermute | solution.py:32
  169.8 1.9 collective-permute-start.15
  171.7 3.4 %collective-permute-start.16 = (bf16[11,32,768]{2,1,0:T(8,128)(2,1)S(1)}, bf16[11,32,768]{2,1,0:T(8,128)(2,1)S(1)}, u32[]{:S(2)}, u32[]{:S(2)}) collective-permute-start(bf16[11,32,768]{2,1,0:T(8,128)(2,1)S(1)} %constant_dynamic-update-slice_fusion), channel_id=1, source_target_pairs={{0,2},{2,4},{4,6},{6,8},{8,10},{10,12},{12,14},{14,16},{16,18},{18... | collective-permute-start | bytes 1622024 | tf_op jit(solution)/shard_map/ppermute | solution.py:32
  175.9 5.0 %collective-permute-done.15 = bf16[10,32,768]{2,1,0:T(8,128)(2,1)S(1)} collective-permute-done((bf16[10,32,768]{2,1,0:T(8,128)(2,1)S(1)}, bf16[10,32,768]{2,1,0:T(8,128)(2,1)S(1)}, u32[]{:S(2)}, u32[]{:S(2)}) %collective-permute-start.15) | collective-permute-done | bytes 491552 | tf_op jit(solution)/shard_map/ppermute | solution.py:32
  181.8 1.8 collective-permute-done.16
  184.5 16.8 %collective-permute-start.17 = (bf16[768,768]{1,0:T(8,128)(2,1)S(1)}, bf16[768,768]{1,0:T(8,128)(2,1)S(1)}, u32[]{:S(2)}, u32[]{:S(2)}) collective-permute-start(bf16[768,768]{1,0:T(8,128)(2,1)S(1)} %fusion.own_ref), channel_id=1, source_target_pairs={{0,1},{1,0},{2,3},{3,2},{4,5},{5,4},{6,7},{7,6},{8,9},{9,8},{10,11... | collective-permute-start | bytes 3538952 | tf_op jit(solution)/shard_map/ppermute | solution.py:36
  204.7 5.6 %newton.1 = f32[32,768]{1,0:T(8,128)} custom-call(f32[32,768]{1,0:T(8,128)} %get-tuple-element.20.velocity_ref, bf16[768,768]{1,0:T(8,128)(2,1)} %copy-done.1, bf16[768,768]{1,0:T(8,128)(2,1)} %copy-done.2), custom_call_target="tpu_custom_call" | custom-call | tf_op jit(solution)/shard_map/newton/pallas_call | solution.py:228
  (52 shorter events, 14.4 us)
Async XLA Ops:
  4.8 17.9 %copy-start.3 = (bf16[1,1,16,24,768]{4,3,2,1,0:T(8,128)(2,1)S(1)}, bf16[1,1,16,24,768]{4,3,2,1,0:T(8,128)(2,1)}, u32[]{:S(2)}) copy-start(bf16[1,1,16,24,768]{4,3,2,1,0:T(8,128)(2,1)} %param.9) | copy-start | bytes 1769476
  4.8 20.2 %copy-start.5 = (s32[32]{0:T(128)S(1)}, s32[32]{0:T(128)}, u32[]{:S(2)}) copy-start(s32[32]{0:T(128)} %constant.34) | copy-start | bytes 388
  4.8 40.2 %all-to-all-start = ((bf16[32,24,1024]{2,1,0:T(8,128)(2,1)}), bf16[32,24,1024]{2,1,0:T(8,128)(2,1)S(1)}, u32[]{:S(2)}, u32[]{:S(2)}) async-start(bf16[32,24,1024]{2,1,0:T(8,128)(2,1)} %route.1), calls=%async_computation | async-start | bytes 3145728 | tf_op jit(solution)/shard_map/all_to_all | solution.py:190
  22.7 3.9 %collective-permute-start = (bf16[16,24,768]{2,1,0:T(8,128)(2,1)S(1)}, bf16[16,24,768]{2,1,0:T(8,128)(2,1)S(1)}, u32[]{:S(2)}, u32[]{:S(2)}) collective-permute-start(bf16[16,24,768]{2,1,0:T(8,128)(2,1)S(1)} %bitcast.75), channel_id=1, source_target_pairs={{0,1},{1,0},{2,3},{3,2},{4,5},{5,4},{6,7},{7,6},{8,9},{9,8},{10,11... | collective-permute-start | bytes 1769480 | tf_op jit(solution)/shard_map/ppermute | solution.py:36
  45.0 1.2 copy-start
  50.8 20.0 %collective-permute-start.1 = (bf16[11,32,768]{2,1,0:T(8,128)(2,1)}, bf16[11,32,768]{2,1,0:T(8,128)(2,1)S(1)}, u32[]{:S(2)}, u32[]{:S(2)}) collective-permute-start(bf16[11,32,768]{2,1,0:T(8,128)(2,1)} %get-tuple-element.11), channel_id=1, source_target_pairs={{0,2},{2,4},{4,6},{6,8},{8,10},{10,12},{12,14},{14,16},{16,18},{18... | collective-permute-start | bytes 1622024 | tf_op jit(solution)/shard_map/ppermute | solution.py:32
  52.7 19.4 %collective-permute-start.2 = (bf16[10,32,768]{2,1,0:T(8,128)(2,1)}, bf16[10,32,768]{2,1,0:T(8,128)(2,1)S(1)}, u32[]{:S(2)}, u32[]{:S(2)}) collective-permute-start(bf16[10,32,768]{2,1,0:T(8,128)(2,1)} %get-tuple-element.12), channel_id=1, source_target_pairs={{0,62},{2,0},{4,2},{6,4},{8,6},{10,8},{12,10},{14,12},{16,14},{18,... | collective-permute-start | bytes 1474568 | tf_op jit(solution)/shard_map/ppermute | solution.py:32
  72.4 8.4 %collective-permute-start.4 = (bf16[32,768]{1,0:T(8,128)(2,1)S(1)}, bf16[32,768]{1,0:T(8,128)(2,1)S(1)}, u32[]{:S(2)}, u32[]{:S(2)}) collective-permute-start(bf16[32,768]{1,0:T(8,128)(2,1)S(1)} %get-tuple-element.27), channel_id=1, source_target_pairs={{0,6},{2,8},{4,10},{6,12},{8,14},{10,16},{12,18},{14,20},{16,22},{... | collective-permute-start | bytes 147464 | tf_op jit(solution)/shard_map/ppermute | solution.py:32
  74.4 7.5 %collective-permute-start.3 = (bf16[32,768]{1,0:T(8,128)(2,1)S(1)}, bf16[32,768]{1,0:T(8,128)(2,1)S(1)}, u32[]{:S(2)}, u32[]{:S(2)}) collective-permute-start(bf16[32,768]{1,0:T(8,128)(2,1)S(1)} %get-tuple-element.29), channel_id=1, source_target_pairs={{0,58},{2,60},{4,62},{6,0},{8,2},{10,4},{12,6},{14,8},{16,10},{18,... | collective-permute-start | bytes 147464 | tf_op jit(solution)/shard_map/ppermute | solution.py:32
  80.8 40.4 %copy-start.4 = (f32[1,32,768]{2,1,0:T(8,128)S(1)}, f32[1,32,768]{2,1,0:T(8,128)}, u32[]{:S(2)}) copy-start(f32[1,32,768]{2,1,0:T(8,128)} %param.10) | copy-start | bytes 294916
  82.0 10.9 %collective-permute-start.5 = (bf16[3,32,768]{2,1,0:T(8,128)(2,1)S(1)}, bf16[3,32,768]{2,1,0:T(8,128)(2,1)S(1)}, u32[]{:S(2)}, u32[]{:S(2)}) collective-permute-start(bf16[3,32,768]{2,1,0:T(8,128)(2,1)S(1)} %get-tuple-element.13), channel_id=1, source_target_pairs={{0,58},{2,60},{4,62},{6,0},{8,2},{10,4},{12,6},{14,8},{16,10},{18,... | collective-permute-start | bytes 442376 | tf_op jit(solution)/shard_map/ppermute | solution.py:32
  88.8 11.6 %collective-permute-start.6 = (bf16[3,32,768]{2,1,0:T(8,128)(2,1)S(1)}, bf16[3,32,768]{2,1,0:T(8,128)(2,1)S(1)}, u32[]{:S(2)}, u32[]{:S(2)}) collective-permute-start(bf16[3,32,768]{2,1,0:T(8,128)(2,1)S(1)} %get-tuple-element.14), channel_id=1, source_target_pairs={{0,6},{2,8},{4,10},{6,12},{8,14},{10,16},{12,18},{14,20},{16,22},{... | collective-permute-start | bytes 442376 | tf_op jit(solution)/shard_map/ppermute | solution.py:32
  100.5 15.5 %collective-permute-start.7 = (bf16[32,768]{1,0:T(8,128)(2,1)S(1)}, bf16[32,768]{1,0:T(8,128)(2,1)S(1)}, u32[]{:S(2)}, u32[]{:S(2)}) collective-permute-start(bf16[32,768]{1,0:T(8,128)(2,1)S(1)} %get-tuple-element.16), channel_id=1, source_target_pairs={{0,46},{2,48},{4,50},{6,52},{8,54},{10,56},{12,58},{14,60},{16,62}... | collective-permute-start | bytes 147464 | tf_op jit(solution)/shard_map/ppermute | solution.py:32
  105.5 15.7 %collective-permute-start.8 = (bf16[32,768]{1,0:T(8,128)(2,1)S(1)}, bf16[32,768]{1,0:T(8,128)(2,1)S(1)}, u32[]{:S(2)}, u32[]{:S(2)}) collective-permute-start(bf16[32,768]{1,0:T(8,128)(2,1)S(1)} %get-tuple-element.17), channel_id=1, source_target_pairs={{0,18},{2,20},{4,22},{6,24},{8,26},{10,28},{12,30},{14,32},{16,34}... | collective-permute-start | bytes 147464 | tf_op jit(solution)/shard_map/ppermute | solution.py:32
  121.8 16.1 %collective-permute-start.10 = (bf16[32,768]{1,0:T(8,128)(2,1)S(1)}, bf16[32,768]{1,0:T(8,128)(2,1)S(1)}, u32[]{:S(2)}, u32[]{:S(2)}) collective-permute-start(bf16[32,768]{1,0:T(8,128)(2,1)S(1)} %get-tuple-element.19), channel_id=1, source_target_pairs={{0,18},{2,20},{4,22},{6,24},{8,26},{10,28},{12,30},{14,32},{16,34}... | collective-permute-start | bytes 147464 | tf_op jit(solution)/shard_map/ppermute | solution.py:32
  131.1 15.9 %collective-permute-start.9 = (bf16[32,768]{1,0:T(8,128)(2,1)S(1)}, bf16[32,768]{1,0:T(8,128)(2,1)S(1)}, u32[]{:S(2)}, u32[]{:S(2)}) collective-permute-start(bf16[32,768]{1,0:T(8,128)(2,1)S(1)} %get-tuple-element.19), channel_id=1, source_target_pairs={{0,46},{2,48},{4,50},{6,52},{8,54},{10,56},{12,58},{14,60},{16,62}... | collective-permute-start | bytes 147464 | tf_op jit(solution)/shard_map/ppermute | solution.py:32
  147.0 10.6 %collective-permute-start.12 = (bf16[3,32,768]{2,1,0:T(8,128)(2,1)S(1)}, bf16[3,32,768]{2,1,0:T(8,128)(2,1)S(1)}, u32[]{:S(2)}, u32[]{:S(2)}) collective-permute-start(bf16[3,32,768]{2,1,0:T(8,128)(2,1)S(1)} %pad_maximum_fusion.4), channel_id=1, source_target_pairs={{0,6},{2,8},{4,10},{6,12},{8,14},{10,16},{12,18},{14,20},{16,22},{... | collective-permute-start | bytes 442376 | tf_op jit(solution)/shard_map/ppermute | solution.py:32
  148.9 10.6 %collective-permute-start.11 = (bf16[3,32,768]{2,1,0:T(8,128)(2,1)S(1)}, bf16[3,32,768]{2,1,0:T(8,128)(2,1)S(1)}, u32[]{:S(2)}, u32[]{:S(2)}) collective-permute-start(bf16[3,32,768]{2,1,0:T(8,128)(2,1)S(1)} %pad_maximum_fusion.4), channel_id=1, source_target_pairs={{0,58},{2,60},{4,62},{6,0},{8,2},{10,4},{12,6},{14,8},{16,10},{18,... | collective-permute-start | bytes 442376 | tf_op jit(solution)/shard_map/ppermute | solution.py:32
  157.6 12.2 %collective-permute-start.13 = (bf16[1,32,768]{2,1,0:T(8,128)(2,1)S(1)}, bf16[1,32,768]{2,1,0:T(8,128)(2,1)S(1)}, u32[]{:S(2)}, u32[]{:S(2)}) collective-permute-start(bf16[1,32,768]{2,1,0:T(8,128)(2,1)S(1)} %slice.94), channel_id=1, source_target_pairs={{0,6},{2,8},{4,10},{6,12},{8,14},{10,16},{12,18},{14,20},{16,22},{... | collective-permute-start | bytes 147464 | tf_op jit(solution)/shard_map/ppermute | solution.py:32
  159.5 10.2 %collective-permute-start.14 = (bf16[1,32,768]{2,1,0:T(8,128)(2,1)S(1)}, bf16[1,32,768]{2,1,0:T(8,128)(2,1)S(1)}, u32[]{:S(2)}, u32[]{:S(2)}) collective-permute-start(bf16[1,32,768]{2,1,0:T(8,128)(2,1)S(1)} %slice.95), channel_id=1, source_target_pairs={{0,58},{2,60},{4,62},{6,0},{8,2},{10,4},{12,6},{14,8},{16,10},{18,... | collective-permute-start | bytes 147464 | tf_op jit(solution)/shard_map/ppermute | solution.py:32
  169.8 11.2 %collective-permute-start.15 = (bf16[10,32,768]{2,1,0:T(8,128)(2,1)S(1)}, bf16[10,32,768]{2,1,0:T(8,128)(2,1)S(1)}, u32[]{:S(2)}, u32[]{:S(2)}) collective-permute-start(bf16[10,32,768]{2,1,0:T(8,128)(2,1)S(1)} %slice.96), channel_id=1, source_target_pairs={{0,62},{2,0},{4,2},{6,4},{8,6},{10,8},{12,10},{14,12},{16,14},{18,... | collective-permute-start | bytes 1474568 | tf_op jit(solution)/shard_map/ppermute | solution.py:32
  171.7 11.8 %collective-permute-start.16 = (bf16[11,32,768]{2,1,0:T(8,128)(2,1)S(1)}, bf16[11,32,768]{2,1,0:T(8,128)(2,1)S(1)}, u32[]{:S(2)}, u32[]{:S(2)}) collective-permute-start(bf16[11,32,768]{2,1,0:T(8,128)(2,1)S(1)} %constant_dynamic-update-slice_fusion), channel_id=1, source_target_pairs={{0,2},{2,4},{4,6},{6,8},{8,10},{10,12},{12,14},{14,16},{16,18},{18... | collective-permute-start | bytes 1622024 | tf_op jit(solution)/shard_map/ppermute | solution.py:32
  184.5 19.2 %copy-start.1 = (bf16[768,768]{1,0:T(8,128)(2,1)}, bf16[768,768]{1,0:T(8,128)(2,1)S(1)}, u32[]{:S(2)}) copy-start(bf16[768,768]{1,0:T(8,128)(2,1)S(1)} %fusion.own_ref) | copy-start | bytes 3538948
  184.5 19.2 %collective-permute-start.17 = (bf16[768,768]{1,0:T(8,128)(2,1)S(1)}, bf16[768,768]{1,0:T(8,128)(2,1)S(1)}, u32[]{:S(2)}, u32[]{:S(2)}) collective-permute-start(bf16[768,768]{1,0:T(8,128)(2,1)S(1)} %fusion.own_ref), channel_id=1, source_target_pairs={{0,1},{1,0},{2,3},{3,2},{4,5},{5,4},{6,7},{7,6},{8,9},{9,8},{10,11... | collective-permute-start | bytes 3538952 | tf_op jit(solution)/shard_map/ppermute | solution.py:36
  203.7 1.0 copy-start.2

commit v4 on v3

--- a/solution.py
+++ b/solution.py
@@ -6,6 +6,7 @@
 from jax.sharding import Mesh
 from jax.sharding import PartitionSpec as P
 
+
 D = 2048
 FSDP = ("z", "core")
 EXPERT_FSDP = ("expert", "z", "core")
@@ -21,6 +22,8 @@
 STEPS = BASE + ABOVE + BELOW + (-5, 5)
 UP = STEPS[:-1]
 DOWN = STEPS
+REACH = 5
+NARROW = (5, 4, 3)
 OFFSETS = (
     tuple(STRIDE * a + 1 for a in UP)
     + tuple(STRIDE * a - 1 for a in DOWN)
@@ -129,26 +132,30 @@
     out_ref[...] = final * jnp.sqrt(jnp.float32(D))
 
 
+def after(x, earlier):
+    return lax.optimization_barrier((x, earlier))[0]
+
+
 def reduce_over_ring(up, down, middle, ring):
     f32, bf16 = jnp.float32, jnp.bfloat16
     up = shifted(up, -1, ring)
     down = shifted(down, 1, ring)
-    sums = middle + down.astype(f32)
-    sums = jnp.concatenate([sums[:-1] + up.astype(f32), sums[-1:]])
+    sums = {}
+    for n, a in enumerate(STEPS):
+        sums[a] = middle[n] + down[n].astype(f32)
+        if a in UP:
+            sums[a] = sums[a] + up[n].astype(f32)
     sums = lax.optimization_barrier(sums)
-    base, above, below = sums[0:3], sums[3:6], sums[6:9]
-    up = shifted(sums[10].astype(bf16), -STRIDE, ring).astype(f32)
-    down = shifted(sums[9].astype(bf16), STRIDE, ring).astype(f32)
-    above = jnp.stack([above[0], above[1] + up, above[2]]).astype(bf16)
-    below = jnp.stack([below[0], below[1], below[2] + down]).astype(bf16)
-    above, below = lax.optimization_barrier((above, below))
-    up = shifted(above, -STRIDE, ring)
-    down = shifted(below, STRIDE, ring)
-    base = base + up.astype(f32) + down.astype(f32)
-    far = lax.optimization_barrier((base[0], base[1].astype(bf16), base[2].astype(bf16)))
-    up = shifted(far[1], -3 * STRIDE, ring)
-    down = shifted(far[2], 3 * STRIDE, ring)
-    return far[0] + up.astype(f32) + down.astype(f32)
+    got = {}
+    last = None
+    for k in range(REACH, 0, -1):
+        for side in (1, -1):
+            total = sums[side * k]
+            if side in got:
+                total = total + after(got[side], last).astype(f32)
+            last = total.astype(bf16) if k in NARROW else total
+            got[side] = shifted(last, -side * STRIDE, ring)
+    return sums[0] + got[1] + got[-1]
 
 
 def gram_of(blocks):

time: 214 us -> 220 us (1.028)
  starting transfers between devices: 118 us -> 128 us
  waiting for transfers between devices: 67.4 us -> 62.2 us
    ppermute x16 -> x20, starting transfers between devices: 80.9 us -> 90.2 us  [shifted(): return lax.ppermute(x, 'z', [(i, (i + by) % ring) for i in range(ring)])]
    ppermute x16 -> x20, waiting for transfers between devices: 47.4 us -> 42.2 us  [shifted(): return lax.ppermute(x, 'z', [(i, (i + by) % ring) for i in range(ring)])]
  transfers between devices with their start and end apart: 19 -> 23, of which waited for: 15 -> 14; matrix products, arithmetic and copies ran while one was open for 3% -> 2% of each run, Pallas kernels for 0% -> 0%
where the time goes in v4:
time: 220 us; the launch traced here: 216 us
  starting transfers between devices  128 us (58%)
  waiting for transfers between devices  62.2 us (28%)
  Pallas kernels  14.4 us (7%)
  other arithmetic  4.24 us (2%)
  local copies, waits for them, and re-layouts  3.41 us (2%)
  matrix products  2.48 us (1%)
    ppermute x20, starting transfers between devices, shifted(): return lax.ppermute(x, 'z', [(i, (i + by) % ring) for i in range(ring)])  90.2 us
    ppermute x20, waiting for transfers between devices, shifted(): return lax.ppermute(x, 'z', [(i, (i + by) % ring) for i in range(ring)])  42.2 us
    ppermute x2, starting transfers between devices, swapped(): return lax.ppermute(x, 'core', [(0, 1), (1, 0)])  19.9 us
    all_to_all x1, starting transfers between devices, local(): lax.all_to_all(outgoing, ('expert', 'core'), split_axis=0, concat_axis=0,...  17.9 us
    all_to_all x1, waiting for transfers between devices, local(): lax.all_to_all(outgoing, ('expert', 'core'), split_axis=0, concat_axis=0,...  17.1 us
    pallas_call x1, Pallas kernels, local(): pl.pallas_call(newton_kernel, out_shape=jax.ShapeDtypeStruct((d_local, un...  5.63 us
    pallas_call x1, Pallas kernels, local(): pl.pallas_call(partial_kernel, out_shape=(jax.ShapeDtypeStruct((len(UP),...  4.58 us
  transfers between devices with their start and end apart: 23, of which 14 were waited for; matrix products, arithmetic and copies ran while one was open for 2% of the time, Pallas kernels for 0%

profile of v4, /device:TPU:1, one launch (start us, length us, event | category | flops | bytes accessed | tf_op | source)
XLA Modules:
  0.0 215.8 jit_solution(8480973056193083398)
XLA Ops:
  0.6 4.2 %route.1 = bf16[32,24,1024]{2,1,0:T(8,128)(2,1)} custom-call(s32[1,256]{1,0:T(1,128)} %bitcast.72, f32[1,256]{1,0:T(1,128)} %bitcast.73, bf16[256,2048]{1,0:T(8,128)(2,1)} %refs_2_.1), custom_call_target="tpu_custom_call" | custom-call | tf_op jit(solution)/shard_map/route/pallas_call | solution.py:192
  4.8 17.9 %all-to-all-start = ((bf16[32,24,1024]{2,1,0:T(8,128)(2,1)}), bf16[32,24,1024]{2,1,0:T(8,128)(2,1)S(1)}, u32[]{:S(2)}, u32[]{:S(2)}) async-start(bf16[32,24,1024]{2,1,0:T(8,128)(2,1)} %route.1), calls=%async_computation | async-start | bytes 3145728 | tf_op jit(solution)/shard_map/all_to_all | solution.py:197
  22.7 2.3 %collective-permute-start = (bf16[16,24,768]{2,1,0:T(8,128)(2,1)S(1)}, bf16[16,24,768]{2,1,0:T(8,128)(2,1)S(1)}, u32[]{:S(2)}, u32[]{:S(2)}) collective-permute-start(bf16[16,24,768]{2,1,0:T(8,128)(2,1)S(1)} %bitcast.67), channel_id=1, source_target_pairs={{0,1},{1,0},{2,3},{3,2},{4,5},{5,4},{6,7},{7,6},{8,9},{9,8},{10,11... | collective-permute-start | bytes 1769480 | tf_op jit(solution)/shard_map/ppermute | solution.py:39
  27.9 17.1 %all-to-all-done = bf16[32,24,1024]{2,1,0:T(8,128)(2,1)S(1)} async-done(((bf16[32,24,1024]{2,1,0:T(8,128)(2,1)}), bf16[32,24,1024]{2,1,0:T(8,128)(2,1)S(1)}, u32[]{:S(2)}, u32[]{:S(2)}) %all-to-all-start) | async-done | bytes 1572896 | tf_op jit(solution)/shard_map/all_to_all | solution.py:197
  46.2 4.6 %partial.1 = (bf16[10,32,768]{2,1,0:T(8,128)(2,1)}, bf16[11,32,768]{2,1,0:T(8,128)(2,1)}, f32[11,32,768]{2,1,0:T(8,128)}) custom-call(s32[32]{0:T(128)} %and_select_fusion.chunk_ref, bf16[768,1024]{1,0:T(8,128)(2,1)} %bitcast.65, bf16[768,768]{1,0:T(8,128)(2,1)} %bitcast.66), custom_call_target="tpu_custom_call" | custom-call | tf_op jit(solution)/shard_map/partial/pallas_call | solution.py:210
  50.8 2.0 collective-permute-start.1
  52.8 9.1 %collective-permute-start.2 = (bf16[10,32,768]{2,1,0:T(8,128)(2,1)}, bf16[10,32,768]{2,1,0:T(8,128)(2,1)S(1)}, u32[]{:S(2)}, u32[]{:S(2)}) collective-permute-start(bf16[10,32,768]{2,1,0:T(8,128)(2,1)} %get-tuple-element.26), channel_id=1, source_target_pairs={{0,62},{2,0},{4,2},{6,4},{8,6},{10,8},{12,10},{14,12},{16,14},{18,... | collective-permute-start | bytes 1474568 | tf_op jit(solution)/shard_map/ppermute | solution.py:35
  61.9 8.9 %collective-permute-done.2 = bf16[10,32,768]{2,1,0:T(8,128)(2,1)S(1)} collective-permute-done((bf16[10,32,768]{2,1,0:T(8,128)(2,1)}, bf16[10,32,768]{2,1,0:T(8,128)(2,1)S(1)}, u32[]{:S(2)}, u32[]{:S(2)}) %collective-permute-start.2) | collective-permute-done | bytes 491552 | tf_op jit(solution)/shard_map/ppermute | solution.py:35
  73.0 5.4 %collective-permute-start.3 = (bf16[32,768]{1,0:T(8,128)(2,1)S(1)}, bf16[32,768]{1,0:T(8,128)(2,1)S(1)}, u32[]{:S(2)}, u32[]{:S(2)}) collective-permute-start(bf16[32,768]{1,0:T(8,128)(2,1)S(1)} %get-tuple-element.32), channel_id=1, source_target_pairs={{0,58},{2,60},{4,62},{6,0},{8,2},{10,4},{12,6},{14,8},{16,10},{18,... | collective-permute-start | bytes 147464 | tf_op jit(solution)/shard_map/ppermute | solution.py:35
  78.4 1.9 collective-permute-start.5
  80.4 6.4 %collective-permute-start.4 = (bf16[32,768]{1,0:T(8,128)(2,1)S(1)}, bf16[32,768]{1,0:T(8,128)(2,1)S(1)}, u32[]{:S(2)}, u32[]{:S(2)}) collective-permute-start(bf16[32,768]{1,0:T(8,128)(2,1)S(1)} %add_convert_fusion.3), channel_id=1, source_target_pairs={{0,58},{2,60},{4,62},{6,0},{8,2},{10,4},{12,6},{14,8},{16,10},{18,... | collective-permute-start | bytes 147464 | tf_op jit(solution)/shard_map/ppermute | solution.py:35
  86.8 1.9 collective-permute-start.7
  88.8 6.4 %collective-permute-start.6 = (bf16[32,768]{1,0:T(8,128)(2,1)S(1)}, bf16[32,768]{1,0:T(8,128)(2,1)S(1)}, u32[]{:S(2)}, u32[]{:S(2)}) collective-permute-start(bf16[32,768]{1,0:T(8,128)(2,1)S(1)} %add_convert_fusion.1), channel_id=1, source_target_pairs={{0,58},{2,60},{4,62},{6,0},{8,2},{10,4},{12,6},{14,8},{16,10},{18,... | collective-permute-start | bytes 147464 | tf_op jit(solution)/shard_map/ppermute | solution.py:35
  95.2 1.9 collective-permute-start.9
  97.1 6.4 %collective-permute-start.8 = (f32[32,768]{1,0:T(8,128)S(1)}, f32[32,768]{1,0:T(8,128)S(1)}, u32[]{:S(2)}, u32[]{:S(2)}) collective-permute-start(f32[32,768]{1,0:T(8,128)S(1)} %convert_add_fusion.1), channel_id=1, source_target_pairs={{0,58},{2,60},{4,62},{6,0},{8,2},{10,4},{12,6},{14,8},{16,10},{18,... | collective-permute-start | bytes 294920 | tf_op jit(solution)/shard_map/ppermute | solution.py:35
  103.5 1.9 collective-permute-start.11
  106.5 5.8 %collective-permute-done.11 = f32[32,768]{1,0:T(8,128)S(1)} collective-permute-done((f32[32,768]{1,0:T(8,128)S(1)}, f32[32,768]{1,0:T(8,128)S(1)}, u32[]{:S(2)}, u32[]{:S(2)}) %collective-permute-start.11) | collective-permute-done | bytes 98336 | tf_op jit(solution)/shard_map/ppermute | solution.py:35
  112.3 1.9 collective-permute-start.12
  114.2 6.4 %collective-permute-start.10 = (f32[32,768]{1,0:T(8,128)S(1)}, f32[32,768]{1,0:T(8,128)S(1)}, u32[]{:S(2)}, u32[]{:S(2)}) collective-permute-start(f32[32,768]{1,0:T(8,128)S(1)} %add.193), channel_id=1, source_target_pairs={{0,58},{2,60},{4,62},{6,0},{8,2},{10,4},{12,6},{14,8},{16,10},{18,... | collective-permute-start | bytes 294920 | tf_op jit(solution)/shard_map/ppermute | solution.py:35
  122.9 9.4 %collective-permute-start.14 = (bf16[32,768]{1,0:T(8,128)(2,1)S(1)}, bf16[32,768]{1,0:T(8,128)(2,1)S(1)}, u32[]{:S(2)}, u32[]{:S(2)}) collective-permute-start(bf16[32,768]{1,0:T(8,128)(2,1)S(1)} %get-tuple-element.47), channel_id=1, source_target_pairs={{0,18},{2,20},{4,22},{6,24},{8,26},{10,28},{12,30},{14,32},{16,34}... | collective-permute-start | bytes 147464 | tf_op jit(solution)/shard_map/ppermute | solution.py:35
  132.3 7.3 %collective-permute-start.13 = (bf16[32,768]{1,0:T(8,128)(2,1)S(1)}, bf16[32,768]{1,0:T(8,128)(2,1)S(1)}, u32[]{:S(2)}, u32[]{:S(2)}) collective-permute-start(bf16[32,768]{1,0:T(8,128)(2,1)S(1)} %get-tuple-element.47), channel_id=1, source_target_pairs={{0,46},{2,48},{4,50},{6,52},{8,54},{10,56},{12,58},{14,60},{16,62}... | collective-permute-start | bytes 147464 | tf_op jit(solution)/shard_map/ppermute | solution.py:35
  139.6 7.7 %collective-permute-done.13 = bf16[32,768]{1,0:T(8,128)(2,1)S(1)} collective-permute-done((bf16[32,768]{1,0:T(8,128)(2,1)S(1)}, bf16[32,768]{1,0:T(8,128)(2,1)S(1)}, u32[]{:S(2)}, u32[]{:S(2)}) %collective-permute-start.13) | collective-permute-done | bytes 49184 | tf_op jit(solution)/shard_map/ppermute | solution.py:35
  147.3 6.6 %collective-permute-start.16 = (bf16[3,32,768]{2,1,0:T(8,128)(2,1)S(1)}, bf16[3,32,768]{2,1,0:T(8,128)(2,1)S(1)}, u32[]{:S(2)}, u32[]{:S(2)}) collective-permute-start(bf16[3,32,768]{2,1,0:T(8,128)(2,1)S(1)} %pad_maximum_fusion.1), channel_id=1, source_target_pairs={{0,6},{2,8},{4,10},{6,12},{8,14},{10,16},{12,18},{14,20},{16,22},{... | collective-permute-start | bytes 442376 | tf_op jit(solution)/shard_map/ppermute | solution.py:35
  155.9 2.2 %collective-permute-done.16 = bf16[3,32,768]{2,1,0:T(8,128)(2,1)S(1)} collective-permute-done((bf16[3,32,768]{2,1,0:T(8,128)(2,1)S(1)}, bf16[3,32,768]{2,1,0:T(8,128)(2,1)S(1)}, u32[]{:S(2)}, u32[]{:S(2)}) %collective-permute-start.16) | collective-permute-done | bytes 147488 | tf_op jit(solution)/shard_map/ppermute | solution.py:35
  158.1 6.1 %collective-permute-start.17 = (bf16[1,32,768]{2,1,0:T(8,128)(2,1)S(1)}, bf16[1,32,768]{2,1,0:T(8,128)(2,1)S(1)}, u32[]{:S(2)}, u32[]{:S(2)}) collective-permute-start(bf16[1,32,768]{2,1,0:T(8,128)(2,1)S(1)} %slice.161), channel_id=1, source_target_pairs={{0,6},{2,8},{4,10},{6,12},{8,14},{10,16},{12,18},{14,20},{16,22},{... | collective-permute-start | bytes 147464 | tf_op jit(solution)/shard_map/ppermute | solution.py:35
  165.8 2.0 collective-permute-start.18
  167.8 7.0 %collective-permute-done.18 = bf16[1,32,768]{2,1,0:T(8,128)(2,1)S(1)} collective-permute-done((bf16[1,32,768]{2,1,0:T(8,128)(2,1)S(1)}, bf16[1,32,768]{2,1,0:T(8,128)(2,1)S(1)}, u32[]{:S(2)}, u32[]{:S(2)}) %collective-permute-start.18) | collective-permute-done | bytes 49184 | tf_op jit(solution)/shard_map/ppermute | solution.py:35
  174.9 1.9 collective-permute-start.19
  176.8 3.4 %collective-permute-start.20 = (bf16[11,32,768]{2,1,0:T(8,128)(2,1)S(1)}, bf16[11,32,768]{2,1,0:T(8,128)(2,1)S(1)}, u32[]{:S(2)}, u32[]{:S(2)}) collective-permute-start(bf16[11,32,768]{2,1,0:T(8,128)(2,1)S(1)} %constant_dynamic-update-slice_fusion), channel_id=1, source_target_pairs={{0,2},{2,4},{4,6},{6,8},{8,10},{10,12},{12,14},{14,16},{16,18},{18... | collective-permute-start | bytes 1622024 | tf_op jit(solution)/shard_map/ppermute | solution.py:35
  181.0 4.7 %collective-permute-done.19 = bf16[10,32,768]{2,1,0:T(8,128)(2,1)S(1)} collective-permute-done((bf16[10,32,768]{2,1,0:T(8,128)(2,1)S(1)}, bf16[10,32,768]{2,1,0:T(8,128)(2,1)S(1)}, u32[]{:S(2)}, u32[]{:S(2)}) %collective-permute-start.19) | collective-permute-done | bytes 491552 | tf_op jit(solution)/shard_map/ppermute | solution.py:35
  189.0 17.6 %collective-permute-start.21 = (bf16[768,768]{1,0:T(8,128)(2,1)S(1)}, bf16[768,768]{1,0:T(8,128)(2,1)S(1)}, u32[]{:S(2)}, u32[]{:S(2)}) collective-permute-start(bf16[768,768]{1,0:T(8,128)(2,1)S(1)} %fusion.own_ref), channel_id=1, source_target_pairs={{0,1},{1,0},{2,3},{3,2},{4,5},{5,4},{6,7},{7,6},{8,9},{9,8},{10,11... | collective-permute-start | bytes 3538952 | tf_op jit(solution)/shard_map/ppermute | solution.py:39
  210.2 5.6 %newton.1 = f32[32,768]{1,0:T(8,128)} custom-call(f32[32,768]{1,0:T(8,128)} %get-tuple-element.48.velocity_ref, bf16[768,768]{1,0:T(8,128)(2,1)} %copy-done.1, bf16[768,768]{1,0:T(8,128)(2,1)} %copy-done.2), custom_call_target="tpu_custom_call" | custom-call | tf_op jit(solution)/shard_map/newton/pallas_call | solution.py:235
  (61 shorter events, 20.8 us)
Async XLA Ops:
  4.8 17.9 %copy-start.4 = (bf16[1,1,16,24,768]{4,3,2,1,0:T(8,128)(2,1)S(1)}, bf16[1,1,16,24,768]{4,3,2,1,0:T(8,128)(2,1)}, u32[]{:S(2)}) copy-start(bf16[1,1,16,24,768]{4,3,2,1,0:T(8,128)(2,1)} %param.9) | copy-start | bytes 1769476
  4.8 20.2 %copy-start.6 = (s32[32]{0:T(128)S(1)}, s32[32]{0:T(128)}, u32[]{:S(2)}) copy-start(s32[32]{0:T(128)} %constant.34) | copy-start | bytes 388
  4.8 40.2 %all-to-all-start = ((bf16[32,24,1024]{2,1,0:T(8,128)(2,1)}), bf16[32,24,1024]{2,1,0:T(8,128)(2,1)S(1)}, u32[]{:S(2)}, u32[]{:S(2)}) async-start(bf16[32,24,1024]{2,1,0:T(8,128)(2,1)} %route.1), calls=%async_computation | async-start | bytes 3145728 | tf_op jit(solution)/shard_map/all_to_all | solution.py:197
  22.7 3.9 %collective-permute-start = (bf16[16,24,768]{2,1,0:T(8,128)(2,1)S(1)}, bf16[16,24,768]{2,1,0:T(8,128)(2,1)S(1)}, u32[]{:S(2)}, u32[]{:S(2)}) collective-permute-start(bf16[16,24,768]{2,1,0:T(8,128)(2,1)S(1)} %bitcast.67), channel_id=1, source_target_pairs={{0,1},{1,0},{2,3},{3,2},{4,5},{5,4},{6,7},{7,6},{8,9},{9,8},{10,11... | collective-permute-start | bytes 1769480 | tf_op jit(solution)/shard_map/ppermute | solution.py:39
  45.0 1.2 copy-start
  50.8 22.1 %copy-start.3 = (f32[11,32,768]{2,1,0:T(8,128)S(1)}, f32[11,32,768]{2,1,0:T(8,128)}, u32[]{:S(2)}) copy-start(f32[11,32,768]{2,1,0:T(8,128)} %get-tuple-element.24) | copy-start | bytes 3244036
  50.8 20.1 %collective-permute-start.1 = (bf16[11,32,768]{2,1,0:T(8,128)(2,1)}, bf16[11,32,768]{2,1,0:T(8,128)(2,1)S(1)}, u32[]{:S(2)}, u32[]{:S(2)}) collective-permute-start(bf16[11,32,768]{2,1,0:T(8,128)(2,1)} %get-tuple-element.25), channel_id=1, source_target_pairs={{0,2},{2,4},{4,6},{6,8},{8,10},{10,12},{12,14},{14,16},{16,18},{18... | collective-permute-start | bytes 1622024 | tf_op jit(solution)/shard_map/ppermute | solution.py:35
  52.8 18.0 %collective-permute-start.2 = (bf16[10,32,768]{2,1,0:T(8,128)(2,1)}, bf16[10,32,768]{2,1,0:T(8,128)(2,1)S(1)}, u32[]{:S(2)}, u32[]{:S(2)}) collective-permute-start(bf16[10,32,768]{2,1,0:T(8,128)(2,1)} %get-tuple-element.26), channel_id=1, source_target_pairs={{0,62},{2,0},{4,2},{6,4},{8,6},{10,8},{12,10},{14,12},{16,14},{18,... | collective-permute-start | bytes 1474568 | tf_op jit(solution)/shard_map/ppermute | solution.py:35
  73.0 49.2 %copy-start.5 = (f32[1,32,768]{2,1,0:T(8,128)S(1)}, f32[1,32,768]{2,1,0:T(8,128)}, u32[]{:S(2)}) copy-start(f32[1,32,768]{2,1,0:T(8,128)} %param.10) | copy-start | bytes 294916
  73.0 7.4 %collective-permute-start.3 = (bf16[32,768]{1,0:T(8,128)(2,1)S(1)}, bf16[32,768]{1,0:T(8,128)(2,1)S(1)}, u32[]{:S(2)}, u32[]{:S(2)}) collective-permute-start(bf16[32,768]{1,0:T(8,128)(2,1)S(1)} %get-tuple-element.32), channel_id=1, source_target_pairs={{0,58},{2,60},{4,62},{6,0},{8,2},{10,4},{12,6},{14,8},{16,10},{18,... | collective-permute-start | bytes 147464 | tf_op jit(solution)/shard_map/ppermute | solution.py:35
  78.4 8.3 %collective-permute-start.5 = (bf16[32,768]{1,0:T(8,128)(2,1)S(1)}, bf16[32,768]{1,0:T(8,128)(2,1)S(1)}, u32[]{:S(2)}, u32[]{:S(2)}) collective-permute-start(bf16[32,768]{1,0:T(8,128)(2,1)S(1)} %get-tuple-element.33), channel_id=1, source_target_pairs={{0,6},{2,8},{4,10},{6,12},{8,14},{10,16},{12,18},{14,20},{16,22},{... | collective-permute-start | bytes 147464 | tf_op jit(solution)/shard_map/ppermute | solution.py:35
  80.4 8.3 %collective-permute-start.4 = (bf16[32,768]{1,0:T(8,128)(2,1)S(1)}, bf16[32,768]{1,0:T(8,128)(2,1)S(1)}, u32[]{:S(2)}, u32[]{:S(2)}) collective-permute-start(bf16[32,768]{1,0:T(8,128)(2,1)S(1)} %add_convert_fusion.3), channel_id=1, source_target_pairs={{0,58},{2,60},{4,62},{6,0},{8,2},{10,4},{12,6},{14,8},{16,10},{18,... | collective-permute-start | bytes 147464 | tf_op jit(solution)/shard_map/ppermute | solution.py:35
  86.8 8.3 %collective-permute-start.7 = (bf16[32,768]{1,0:T(8,128)(2,1)S(1)}, bf16[32,768]{1,0:T(8,128)(2,1)S(1)}, u32[]{:S(2)}, u32[]{:S(2)}) collective-permute-start(bf16[32,768]{1,0:T(8,128)(2,1)S(1)} %add_convert_fusion.2), channel_id=1, source_target_pairs={{0,6},{2,8},{4,10},{6,12},{8,14},{10,16},{12,18},{14,20},{16,22},{... | collective-permute-start | bytes 147464 | tf_op jit(solution)/shard_map/ppermute | solution.py:35
  88.8 8.3 %collective-permute-start.6 = (bf16[32,768]{1,0:T(8,128)(2,1)S(1)}, bf16[32,768]{1,0:T(8,128)(2,1)S(1)}, u32[]{:S(2)}, u32[]{:S(2)}) collective-permute-start(bf16[32,768]{1,0:T(8,128)(2,1)S(1)} %add_convert_fusion.1), channel_id=1, source_target_pairs={{0,58},{2,60},{4,62},{6,0},{8,2},{10,4},{12,6},{14,8},{16,10},{18,... | collective-permute-start | bytes 147464 | tf_op jit(solution)/shard_map/ppermute | solution.py:35
  95.2 8.3 %collective-permute-start.9 = (bf16[32,768]{1,0:T(8,128)(2,1)S(1)}, bf16[32,768]{1,0:T(8,128)(2,1)S(1)}, u32[]{:S(2)}, u32[]{:S(2)}) collective-permute-start(bf16[32,768]{1,0:T(8,128)(2,1)S(1)} %add_convert_fusion), channel_id=1, source_target_pairs={{0,6},{2,8},{4,10},{6,12},{8,14},{10,16},{12,18},{14,20},{16,22},{... | collective-permute-start | bytes 147464 | tf_op jit(solution)/shard_map/ppermute | solution.py:35
  97.1 9.4 %collective-permute-start.8 = (f32[32,768]{1,0:T(8,128)S(1)}, f32[32,768]{1,0:T(8,128)S(1)}, u32[]{:S(2)}, u32[]{:S(2)}) collective-permute-start(f32[32,768]{1,0:T(8,128)S(1)} %convert_add_fusion.1), channel_id=1, source_target_pairs={{0,58},{2,60},{4,62},{6,0},{8,2},{10,4},{12,6},{14,8},{16,10},{18,... | collective-permute-start | bytes 294920 | tf_op jit(solution)/shard_map/ppermute | solution.py:35
  103.5 8.8 %collective-permute-start.11 = (f32[32,768]{1,0:T(8,128)S(1)}, f32[32,768]{1,0:T(8,128)S(1)}, u32[]{:S(2)}, u32[]{:S(2)}) collective-permute-start(f32[32,768]{1,0:T(8,128)S(1)} %convert_add_fusion), channel_id=1, source_target_pairs={{0,6},{2,8},{4,10},{6,12},{8,14},{10,16},{12,18},{14,20},{16,22},{... | collective-permute-start | bytes 294920 | tf_op jit(solution)/shard_map/ppermute | solution.py:35
  112.3 9.6 %collective-permute-start.12 = (f32[32,768]{1,0:T(8,128)S(1)}, f32[32,768]{1,0:T(8,128)S(1)}, u32[]{:S(2)}, u32[]{:S(2)}) collective-permute-start(f32[32,768]{1,0:T(8,128)S(1)} %add.195), channel_id=1, source_target_pairs={{0,6},{2,8},{4,10},{6,12},{8,14},{10,16},{12,18},{14,20},{16,22},{... | collective-permute-start | bytes 294920 | tf_op jit(solution)/shard_map/ppermute | solution.py:35
  114.2 8.0 %collective-permute-start.10 = (f32[32,768]{1,0:T(8,128)S(1)}, f32[32,768]{1,0:T(8,128)S(1)}, u32[]{:S(2)}, u32[]{:S(2)}) collective-permute-start(f32[32,768]{1,0:T(8,128)S(1)} %add.193), channel_id=1, source_target_pairs={{0,58},{2,60},{4,62},{6,0},{8,2},{10,4},{12,6},{14,8},{16,10},{18,... | collective-permute-start | bytes 294920 | tf_op jit(solution)/shard_map/ppermute | solution.py:35
  122.9 16.7 %collective-permute-start.14 = (bf16[32,768]{1,0:T(8,128)(2,1)S(1)}, bf16[32,768]{1,0:T(8,128)(2,1)S(1)}, u32[]{:S(2)}, u32[]{:S(2)}) collective-permute-start(bf16[32,768]{1,0:T(8,128)(2,1)S(1)} %get-tuple-element.47), channel_id=1, source_target_pairs={{0,18},{2,20},{4,22},{6,24},{8,26},{10,28},{12,30},{14,32},{16,34}... | collective-permute-start | bytes 147464 | tf_op jit(solution)/shard_map/ppermute | solution.py:35
  132.3 15.0 %collective-permute-start.13 = (bf16[32,768]{1,0:T(8,128)(2,1)S(1)}, bf16[32,768]{1,0:T(8,128)(2,1)S(1)}, u32[]{:S(2)}, u32[]{:S(2)}) collective-permute-start(bf16[32,768]{1,0:T(8,128)(2,1)S(1)} %get-tuple-element.47), channel_id=1, source_target_pairs={{0,46},{2,48},{4,50},{6,52},{8,54},{10,56},{12,58},{14,60},{16,62}... | collective-permute-start | bytes 147464 | tf_op jit(solution)/shard_map/ppermute | solution.py:35
  147.3 10.8 %collective-permute-start.16 = (bf16[3,32,768]{2,1,0:T(8,128)(2,1)S(1)}, bf16[3,32,768]{2,1,0:T(8,128)(2,1)S(1)}, u32[]{:S(2)}, u32[]{:S(2)}) collective-permute-start(bf16[3,32,768]{2,1,0:T(8,128)(2,1)S(1)} %pad_maximum_fusion.1), channel_id=1, source_target_pairs={{0,6},{2,8},{4,10},{6,12},{8,14},{10,16},{12,18},{14,20},{16,22},{... | collective-permute-start | bytes 442376 | tf_op jit(solution)/shard_map/ppermute | solution.py:35
  153.9 11.9 %collective-permute-start.15 = (bf16[3,32,768]{2,1,0:T(8,128)(2,1)S(1)}, bf16[3,32,768]{2,1,0:T(8,128)(2,1)S(1)}, u32[]{:S(2)}, u32[]{:S(2)}) collective-permute-start(bf16[3,32,768]{2,1,0:T(8,128)(2,1)S(1)} %pad_maximum_fusion.1), channel_id=1, source_target_pairs={{0,58},{2,60},{4,62},{6,0},{8,2},{10,4},{12,6},{14,8},{16,10},{18,... | collective-permute-start | bytes 442376 | tf_op jit(solution)/shard_map/ppermute | solution.py:35
  158.1 9.7 %collective-permute-start.17 = (bf16[1,32,768]{2,1,0:T(8,128)(2,1)S(1)}, bf16[1,32,768]{2,1,0:T(8,128)(2,1)S(1)}, u32[]{:S(2)}, u32[]{:S(2)}) collective-permute-start(bf16[1,32,768]{2,1,0:T(8,128)(2,1)S(1)} %slice.161), channel_id=1, source_target_pairs={{0,6},{2,8},{4,10},{6,12},{8,14},{10,16},{12,18},{14,20},{16,22},{... | collective-permute-start | bytes 147464 | tf_op jit(solution)/shard_map/ppermute | solution.py:35
  165.8 9.1 %collective-permute-start.18 = (bf16[1,32,768]{2,1,0:T(8,128)(2,1)S(1)}, bf16[1,32,768]{2,1,0:T(8,128)(2,1)S(1)}, u32[]{:S(2)}, u32[]{:S(2)}) collective-permute-start(bf16[1,32,768]{2,1,0:T(8,128)(2,1)S(1)} %slice.162), channel_id=1, source_target_pairs={{0,58},{2,60},{4,62},{6,0},{8,2},{10,4},{12,6},{14,8},{16,10},{18,... | collective-permute-start | bytes 147464 | tf_op jit(solution)/shard_map/ppermute | solution.py:35
  174.9 10.9 %collective-permute-start.19 = (bf16[10,32,768]{2,1,0:T(8,128)(2,1)S(1)}, bf16[10,32,768]{2,1,0:T(8,128)(2,1)S(1)}, u32[]{:S(2)}, u32[]{:S(2)}) collective-permute-start(bf16[10,32,768]{2,1,0:T(8,128)(2,1)S(1)} %slice.163), channel_id=1, source_target_pairs={{0,62},{2,0},{4,2},{6,4},{8,6},{10,8},{12,10},{14,12},{16,14},{18,... | collective-permute-start | bytes 1474568 | tf_op jit(solution)/shard_map/ppermute | solution.py:35
  176.8 11.3 %collective-permute-start.20 = (bf16[11,32,768]{2,1,0:T(8,128)(2,1)S(1)}, bf16[11,32,768]{2,1,0:T(8,128)(2,1)S(1)}, u32[]{:S(2)}, u32[]{:S(2)}) collective-permute-start(bf16[11,32,768]{2,1,0:T(8,128)(2,1)S(1)} %constant_dynamic-update-slice_fusion), channel_id=1, source_target_pairs={{0,2},{2,4},{4,6},{6,8},{8,10},{10,12},{12,14},{14,16},{16,18},{18... | collective-permute-start | bytes 1622024 | tf_op jit(solution)/shard_map/ppermute | solution.py:35
  189.0 20.1 %copy-start.1 = (bf16[768,768]{1,0:T(8,128)(2,1)}, bf16[768,768]{1,0:T(8,128)(2,1)S(1)}, u32[]{:S(2)}) copy-start(bf16[768,768]{1,0:T(8,128)(2,1)S(1)} %fusion.own_ref) | copy-start | bytes 3538948
  189.0 20.1 %collective-permute-start.21 = (bf16[768,768]{1,0:T(8,128)(2,1)S(1)}, bf16[768,768]{1,0:T(8,128)(2,1)S(1)}, u32[]{:S(2)}, u32[]{:S(2)}) collective-permute-start(bf16[768,768]{1,0:T(8,128)(2,1)S(1)} %fusion.own_ref), channel_id=1, source_target_pairs={{0,1},{1,0},{2,3},{3,2},{4,5},{5,4},{6,7},{7,6},{8,9},{9,8},{10,11... | collective-permute-start | bytes 3538952 | tf_op jit(solution)/shard_map/ppermute | solution.py:39
  209.1 1.0 copy-start.2

commit v5 on v3

--- a/solution.py
+++ b/solution.py
@@ -136,15 +136,14 @@
     sums = middle + down.astype(f32)
     sums = jnp.concatenate([sums[:-1] + up.astype(f32), sums[-1:]])
     sums = lax.optimization_barrier(sums)
-    base, above, below = sums[0:3], sums[3:6], sums[6:9]
-    up = shifted(sums[10].astype(bf16), -STRIDE, ring).astype(f32)
-    down = shifted(sums[9].astype(bf16), STRIDE, ring).astype(f32)
-    above = jnp.stack([above[0], above[1] + up, above[2]]).astype(bf16)
-    below = jnp.stack([below[0], below[1], below[2] + down]).astype(bf16)
-    above, below = lax.optimization_barrier((above, below))
-    up = shifted(above, -STRIDE, ring)
-    down = shifted(below, STRIDE, ring)
+    base = sums[0:3]
+    narrow = lax.optimization_barrier(sums[3:].astype(bf16))
+    up = shifted(narrow[0:3], -STRIDE, ring)
+    down = shifted(narrow[3:6], STRIDE, ring)
+    up_twice = shifted(narrow[7], -2 * STRIDE, ring).astype(f32)
+    down_twice = shifted(narrow[6], 2 * STRIDE, ring).astype(f32)
     base = base + up.astype(f32) + down.astype(f32)
+    base = jnp.stack([base[0], base[1] + up_twice, base[2] + down_twice])
     far = lax.optimization_barrier((base[0], base[1].astype(bf16), base[2].astype(bf16)))
     up = shifted(far[1], -3 * STRIDE, ring)
     down = shifted(far[2], 3 * STRIDE, ring)
@@ -162,8 +161,8 @@
     base = jnp.stack([own, shifted(own, -3 * STRIDE, ring), shifted(own, 3 * STRIDE, ring)])
     above = shifted(base, -STRIDE, ring)
     below = shifted(base, STRIDE, ring)
-    up = shifted(above[1:2], -STRIDE, ring)
-    down = shifted(below[2:3], STRIDE, ring)
+    up = shifted(base[1:2], -2 * STRIDE, ring)
+    down = shifted(base[2:3], 2 * STRIDE, ring)
     rows = lax.optimization_barrier(jnp.concatenate([base, above, below, down, up]))
     up = shifted(rows[:-1], -1, ring)
     down = shifted(rows, 1, ring)

time: 214 us -> 210 us (0.981)
  waiting for transfers between devices: 67.4 us -> 61.2 us
    ppermute x16, waiting for transfers between devices: 47.4 us -> 41.2 us  [shifted(): return lax.ppermute(x, 'z', [(i, (i + by) % ring) for i in range(ring)])]
    ppermute x16, starting transfers between devices: 80.9 us -> 87 us  [shifted(): return lax.ppermute(x, 'z', [(i, (i + by) % ring) for i in range(ring)])]
    ppermute x2, starting transfers between devices: 19 us -> 15.4 us  [swapped(): return lax.ppermute(x, 'core', [(0, 1), (1, 0)])]
  transfers between devices with their start and end apart: 19 -> 19, of which waited for: 15 -> 11; matrix products, arithmetic and copies ran while one was open for 3% -> 3% of each run, Pallas kernels for 0% -> 0%
where the time goes in v5:
time: 210 us; the launch traced here: 207 us
  starting transfers between devices  120 us (57%)
  waiting for transfers between devices  61.2 us (29%)
  Pallas kernels  14.4 us (7%)
  other arithmetic  3.65 us (2%)
  local copies, waits for them, and re-layouts  3.53 us (2%)
  matrix products  2.48 us (1%)
    ppermute x16, starting transfers between devices, shifted(): return lax.ppermute(x, 'z', [(i, (i + by) % ring) for i in range(ring)])  87 us
    ppermute x16, waiting for transfers between devices, shifted(): return lax.ppermute(x, 'z', [(i, (i + by) % ring) for i in range(ring)])  41.2 us
    all_to_all x1, starting transfers between devices, local(): lax.all_to_all(outgoing, ('expert', 'core'), split_axis=0, concat_axis=0,...  17.9 us
    all_to_all x1, waiting for transfers between devices, local(): lax.all_to_all(outgoing, ('expert', 'core'), split_axis=0, concat_axis=0,...  17.1 us
    ppermute x2, starting transfers between devices, swapped(): return lax.ppermute(x, 'core', [(0, 1), (1, 0)])  15.4 us
    pallas_call x1, Pallas kernels, local(): pl.pallas_call(newton_kernel, out_shape=jax.ShapeDtypeStruct((d_local, un...  5.63 us
    pallas_call x1, Pallas kernels, local(): pl.pallas_call(partial_kernel, out_shape=(jax.ShapeDtypeStruct((len(UP),...  4.57 us
  transfers between devices with their start and end apart: 19, of which 11 were waited for; matrix products, arithmetic and copies ran while one was open for 3% of the time, Pallas kernels for 0%

profile of v5, /device:TPU:1, one launch (start us, length us, event | category | flops | bytes accessed | tf_op | source)
XLA Modules:
  0.0 206.5 jit_solution(6722521657413463833)
XLA Ops:
  0.6 4.2 %route.1 = bf16[32,24,1024]{2,1,0:T(8,128)(2,1)} custom-call(s32[1,256]{1,0:T(1,128)} %bitcast.70, f32[1,256]{1,0:T(1,128)} %bitcast.71, bf16[256,2048]{1,0:T(8,128)(2,1)} %refs_2_.1), custom_call_target="tpu_custom_call" | custom-call | tf_op jit(solution)/shard_map/route/pallas_call | solution.py:184
  4.8 17.9 %all-to-all-start = ((bf16[32,24,1024]{2,1,0:T(8,128)(2,1)}), bf16[32,24,1024]{2,1,0:T(8,128)(2,1)S(1)}, u32[]{:S(2)}, u32[]{:S(2)}) async-start(bf16[32,24,1024]{2,1,0:T(8,128)(2,1)} %route.1), calls=%async_computation | async-start | bytes 3145728 | tf_op jit(solution)/shard_map/all_to_all | solution.py:189
  22.7 2.3 %collective-permute-start = (bf16[16,24,768]{2,1,0:T(8,128)(2,1)S(1)}, bf16[16,24,768]{2,1,0:T(8,128)(2,1)S(1)}, u32[]{:S(2)}, u32[]{:S(2)}) collective-permute-start(bf16[16,24,768]{2,1,0:T(8,128)(2,1)S(1)} %bitcast.63), channel_id=1, source_target_pairs={{0,1},{1,0},{2,3},{3,2},{4,5},{5,4},{6,7},{7,6},{8,9},{9,8},{10,11... | collective-permute-start | bytes 1769480 | tf_op jit(solution)/shard_map/ppermute | solution.py:36
  26.8 1.1 copy.8
  27.9 17.1 %all-to-all-done = bf16[32,24,1024]{2,1,0:T(8,128)(2,1)S(1)} async-done(((bf16[32,24,1024]{2,1,0:T(8,128)(2,1)}), bf16[32,24,1024]{2,1,0:T(8,128)(2,1)S(1)}, u32[]{:S(2)}, u32[]{:S(2)}) %all-to-all-start) | async-done | bytes 1572896 | tf_op jit(solution)/shard_map/all_to_all | solution.py:189
  45.1 1.2 copy-done
  46.2 4.6 %partial.1 = (bf16[10,32,768]{2,1,0:T(8,128)(2,1)}, bf16[11,32,768]{2,1,0:T(8,128)(2,1)}, f32[11,32,768]{2,1,0:T(8,128)}) custom-call(s32[32]{0:T(128)} %and_select_fusion.chunk_ref, bf16[768,1024]{1,0:T(8,128)(2,1)} %bitcast.61, bf16[768,768]{1,0:T(8,128)(2,1)} %bitcast.62), custom_call_target="tpu_custom_call" | custom-call | tf_op jit(solution)/shard_map/partial/pallas_call | solution.py:202
  50.8 1.9 collective-permute-start.1
  52.7 9.1 %collective-permute-start.2 = (bf16[10,32,768]{2,1,0:T(8,128)(2,1)}, bf16[10,32,768]{2,1,0:T(8,128)(2,1)S(1)}, u32[]{:S(2)}, u32[]{:S(2)}) collective-permute-start(bf16[10,32,768]{2,1,0:T(8,128)(2,1)} %get-tuple-element.10), channel_id=1, source_target_pairs={{0,62},{2,0},{4,2},{6,4},{8,6},{10,8},{12,10},{14,12},{16,14},{18,... | collective-permute-start | bytes 1474568 | tf_op jit(solution)/shard_map/ppermute | solution.py:32
  61.8 9.0 %collective-permute-done.1 = bf16[11,32,768]{2,1,0:T(8,128)(2,1)S(1)} collective-permute-done((bf16[11,32,768]{2,1,0:T(8,128)(2,1)}, bf16[11,32,768]{2,1,0:T(8,128)(2,1)S(1)}, u32[]{:S(2)}, u32[]{:S(2)}) %collective-permute-start.1) | collective-permute-done | bytes 540704 | tf_op jit(solution)/shard_map/ppermute | solution.py:32
  70.8 1.3 convert_add_fusion
  72.4 4.0 %collective-permute-start.3 = (bf16[3,32,768]{2,1,0:T(8,128)(2,1)S(1)}, bf16[3,32,768]{2,1,0:T(8,128)(2,1)S(1)}, u32[]{:S(2)}, u32[]{:S(2)}) collective-permute-start(bf16[3,32,768]{2,1,0:T(8,128)(2,1)S(1)} %get-tuple-element.21), channel_id=1, source_target_pairs={{0,58},{2,60},{4,62},{6,0},{8,2},{10,4},{12,6},{14,8},{16,10},{18,... | collective-permute-start | bytes 442376 | tf_op jit(solution)/shard_map/ppermute | solution.py:32
  76.4 3.1 %collective-permute-start.4 = (bf16[3,32,768]{2,1,0:T(8,128)(2,1)S(1)}, bf16[3,32,768]{2,1,0:T(8,128)(2,1)S(1)}, u32[]{:S(2)}, u32[]{:S(2)}) collective-permute-start(bf16[3,32,768]{2,1,0:T(8,128)(2,1)S(1)} %get-tuple-element.22), channel_id=1, source_target_pairs={{0,6},{2,8},{4,10},{6,12},{8,14},{10,16},{12,18},{14,20},{16,22},{... | collective-permute-start | bytes 442376 | tf_op jit(solution)/shard_map/ppermute | solution.py:32
  79.6 1.9 collective-permute-start.6
  81.5 10.3 %collective-permute-start.5 = (bf16[32,768]{1,0:T(8,128)(2,1)S(1)}, bf16[32,768]{1,0:T(8,128)(2,1)S(1)}, u32[]{:S(2)}, u32[]{:S(2)}) collective-permute-start(bf16[32,768]{1,0:T(8,128)(2,1)S(1)} %get-tuple-element.20), channel_id=1, source_target_pairs={{0,52},{2,54},{4,56},{6,58},{8,60},{10,62},{12,0},{14,2},{16,4},{1... | collective-permute-start | bytes 147464 | tf_op jit(solution)/shard_map/ppermute | solution.py:32
  91.9 5.5 %collective-permute-done.6 = bf16[32,768]{1,0:T(8,128)(2,1)S(1)} collective-permute-done((bf16[32,768]{1,0:T(8,128)(2,1)S(1)}, bf16[32,768]{1,0:T(8,128)(2,1)S(1)}, u32[]{:S(2)}, u32[]{:S(2)}) %collective-permute-start.6) | collective-permute-done | bytes 49184 | tf_op jit(solution)/shard_map/ppermute | solution.py:32
  97.4 11.5 %collective-permute-start.7 = (bf16[32,768]{1,0:T(8,128)(2,1)S(1)}, bf16[32,768]{1,0:T(8,128)(2,1)S(1)}, u32[]{:S(2)}, u32[]{:S(2)}) collective-permute-start(bf16[32,768]{1,0:T(8,128)(2,1)S(1)} %get-tuple-element.12), channel_id=1, source_target_pairs={{0,46},{2,48},{4,50},{6,52},{8,54},{10,56},{12,58},{14,60},{16,62}... | collective-permute-start | bytes 147464 | tf_op jit(solution)/shard_map/ppermute | solution.py:32
  109.0 3.4 %collective-permute-start.8 = (bf16[32,768]{1,0:T(8,128)(2,1)S(1)}, bf16[32,768]{1,0:T(8,128)(2,1)S(1)}, u32[]{:S(2)}, u32[]{:S(2)}) collective-permute-start(bf16[32,768]{1,0:T(8,128)(2,1)S(1)} %get-tuple-element.13), channel_id=1, source_target_pairs={{0,18},{2,20},{4,22},{6,24},{8,26},{10,28},{12,30},{14,32},{16,34}... | collective-permute-start | bytes 147464 | tf_op jit(solution)/shard_map/ppermute | solution.py:32
  112.5 12.4 %collective-permute-done.8 = bf16[32,768]{1,0:T(8,128)(2,1)S(1)} collective-permute-done((bf16[32,768]{1,0:T(8,128)(2,1)S(1)}, bf16[32,768]{1,0:T(8,128)(2,1)S(1)}, u32[]{:S(2)}, u32[]{:S(2)}) %collective-permute-start.8) | collective-permute-done | bytes 49184 | tf_op jit(solution)/shard_map/ppermute | solution.py:32
  125.6 3.0 %collective-permute-start.10 = (bf16[32,768]{1,0:T(8,128)(2,1)S(1)}, bf16[32,768]{1,0:T(8,128)(2,1)S(1)}, u32[]{:S(2)}, u32[]{:S(2)}) collective-permute-start(bf16[32,768]{1,0:T(8,128)(2,1)S(1)} %get-tuple-element.15), channel_id=1, source_target_pairs={{0,18},{2,20},{4,22},{6,24},{8,26},{10,28},{12,30},{14,32},{16,34}... | collective-permute-start | bytes 147464 | tf_op jit(solution)/shard_map/ppermute | solution.py:32
  128.6 13.1 %collective-permute-start.9 = (bf16[32,768]{1,0:T(8,128)(2,1)S(1)}, bf16[32,768]{1,0:T(8,128)(2,1)S(1)}, u32[]{:S(2)}, u32[]{:S(2)}) collective-permute-start(bf16[32,768]{1,0:T(8,128)(2,1)S(1)} %get-tuple-element.15), channel_id=1, source_target_pairs={{0,46},{2,48},{4,50},{6,52},{8,54},{10,56},{12,58},{14,60},{16,62}... | collective-permute-start | bytes 147464 | tf_op jit(solution)/shard_map/ppermute | solution.py:32
  142.1 1.9 collective-permute-start.13
  144.0 10.3 %collective-permute-start.14 = (bf16[1,32,768]{2,1,0:T(8,128)(2,1)S(1)}, bf16[1,32,768]{2,1,0:T(8,128)(2,1)S(1)}, u32[]{:S(2)}, u32[]{:S(2)}) collective-permute-start(bf16[1,32,768]{2,1,0:T(8,128)(2,1)S(1)} %bitcast.64), channel_id=1, source_target_pairs={{0,52},{2,54},{4,56},{6,58},{8,60},{10,62},{12,0},{14,2},{16,4},{1... | collective-permute-start | bytes 147464 | tf_op jit(solution)/shard_map/ppermute | solution.py:32
  154.3 1.9 collective-permute-start.12
  156.3 6.4 %collective-permute-start.11 = (bf16[3,32,768]{2,1,0:T(8,128)(2,1)S(1)}, bf16[3,32,768]{2,1,0:T(8,128)(2,1)S(1)}, u32[]{:S(2)}, u32[]{:S(2)}) collective-permute-start(bf16[3,32,768]{2,1,0:T(8,128)(2,1)S(1)} %pad_maximum_fusion.2), channel_id=1, source_target_pairs={{0,58},{2,60},{4,62},{6,0},{8,2},{10,4},{12,6},{14,8},{16,10},{18,... | collective-permute-start | bytes 442376 | tf_op jit(solution)/shard_map/ppermute | solution.py:32
  162.7 7.4 %collective-permute-done.11 = bf16[3,32,768]{2,1,0:T(8,128)(2,1)S(1)} collective-permute-done((bf16[3,32,768]{2,1,0:T(8,128)(2,1)S(1)}, bf16[3,32,768]{2,1,0:T(8,128)(2,1)S(1)}, u32[]{:S(2)}, u32[]{:S(2)}) %collective-permute-start.11) | collective-permute-done | bytes 147488 | tf_op jit(solution)/shard_map/ppermute | solution.py:32
  170.2 1.9 collective-permute-start.15
  172.1 3.4 %collective-permute-start.16 = (bf16[11,32,768]{2,1,0:T(8,128)(2,1)S(1)}, bf16[11,32,768]{2,1,0:T(8,128)(2,1)S(1)}, u32[]{:S(2)}, u32[]{:S(2)}) collective-permute-start(bf16[11,32,768]{2,1,0:T(8,128)(2,1)S(1)} %constant_dynamic-update-slice_fusion), channel_id=1, source_target_pairs={{0,2},{2,4},{4,6},{6,8},{8,10},{10,12},{12,14},{14,16},{16,18},{18... | collective-permute-start | bytes 1622024 | tf_op jit(solution)/shard_map/ppermute | solution.py:32
  176.3 5.7 %collective-permute-done.15 = bf16[10,32,768]{2,1,0:T(8,128)(2,1)S(1)} collective-permute-done((bf16[10,32,768]{2,1,0:T(8,128)(2,1)S(1)}, bf16[10,32,768]{2,1,0:T(8,128)(2,1)S(1)}, u32[]{:S(2)}, u32[]{:S(2)}) %collective-permute-start.15) | collective-permute-done | bytes 491552 | tf_op jit(solution)/shard_map/ppermute | solution.py:32
  184.3 13.1 %collective-permute-start.17 = (bf16[768,768]{1,0:T(8,128)(2,1)S(1)}, bf16[768,768]{1,0:T(8,128)(2,1)S(1)}, u32[]{:S(2)}, u32[]{:S(2)}) collective-permute-start(bf16[768,768]{1,0:T(8,128)(2,1)S(1)} %fusion.own_ref), channel_id=1, source_target_pairs={{0,1},{1,0},{2,3},{3,2},{4,5},{5,4},{6,7},{7,6},{8,9},{9,8},{10,11... | collective-permute-start | bytes 3538952 | tf_op jit(solution)/shard_map/ppermute | solution.py:36
  198.1 1.8 collective-permute-done.17.other_ref
  200.9 5.6 %newton.1 = f32[32,768]{1,0:T(8,128)} custom-call(f32[32,768]{1,0:T(8,128)} %get-tuple-element.16.velocity_ref, bf16[768,768]{1,0:T(8,128)(2,1)} %copy-done.1, bf16[768,768]{1,0:T(8,128)(2,1)} %copy-done.2), custom_call_target="tpu_custom_call" | custom-call | tf_op jit(solution)/shard_map/newton/pallas_call | solution.py:227
  (48 shorter events, 8.3 us)
Async XLA Ops:
  4.8 17.9 %copy-start.3 = (bf16[1,1,16,24,768]{4,3,2,1,0:T(8,128)(2,1)S(1)}, bf16[1,1,16,24,768]{4,3,2,1,0:T(8,128)(2,1)}, u32[]{:S(2)}) copy-start(bf16[1,1,16,24,768]{4,3,2,1,0:T(8,128)(2,1)} %param.9) | copy-start | bytes 1769476
  4.8 20.2 %copy-start.5 = (s32[32]{0:T(128)S(1)}, s32[32]{0:T(128)}, u32[]{:S(2)}) copy-start(s32[32]{0:T(128)} %constant.34) | copy-start | bytes 388
  4.8 40.2 %all-to-all-start = ((bf16[32,24,1024]{2,1,0:T(8,128)(2,1)}), bf16[32,24,1024]{2,1,0:T(8,128)(2,1)S(1)}, u32[]{:S(2)}, u32[]{:S(2)}) async-start(bf16[32,24,1024]{2,1,0:T(8,128)(2,1)} %route.1), calls=%async_computation | async-start | bytes 3145728 | tf_op jit(solution)/shard_map/all_to_all | solution.py:189
  22.7 3.9 %collective-permute-start = (bf16[16,24,768]{2,1,0:T(8,128)(2,1)S(1)}, bf16[16,24,768]{2,1,0:T(8,128)(2,1)S(1)}, u32[]{:S(2)}, u32[]{:S(2)}) collective-permute-start(bf16[16,24,768]{2,1,0:T(8,128)(2,1)S(1)} %bitcast.63), channel_id=1, source_target_pairs={{0,1},{1,0},{2,3},{3,2},{4,5},{5,4},{6,7},{7,6},{8,9},{9,8},{10,11... | collective-permute-start | bytes 1769480 | tf_op jit(solution)/shard_map/ppermute | solution.py:36
  45.0 1.2 copy-start
  50.8 20.0 %collective-permute-start.1 = (bf16[11,32,768]{2,1,0:T(8,128)(2,1)}, bf16[11,32,768]{2,1,0:T(8,128)(2,1)S(1)}, u32[]{:S(2)}, u32[]{:S(2)}) collective-permute-start(bf16[11,32,768]{2,1,0:T(8,128)(2,1)} %get-tuple-element.9), channel_id=1, source_target_pairs={{0,2},{2,4},{4,6},{6,8},{8,10},{10,12},{12,14},{14,16},{16,18},{18... | collective-permute-start | bytes 1622024 | tf_op jit(solution)/shard_map/ppermute | solution.py:32
  52.7 19.4 %collective-permute-start.2 = (bf16[10,32,768]{2,1,0:T(8,128)(2,1)}, bf16[10,32,768]{2,1,0:T(8,128)(2,1)S(1)}, u32[]{:S(2)}, u32[]{:S(2)}) collective-permute-start(bf16[10,32,768]{2,1,0:T(8,128)(2,1)} %get-tuple-element.10), channel_id=1, source_target_pairs={{0,62},{2,0},{4,2},{6,4},{8,6},{10,8},{12,10},{14,12},{16,14},{18,... | collective-permute-start | bytes 1474568 | tf_op jit(solution)/shard_map/ppermute | solution.py:32
  72.4 52.5 %copy-start.4 = (f32[1,32,768]{2,1,0:T(8,128)S(1)}, f32[1,32,768]{2,1,0:T(8,128)}, u32[]{:S(2)}) copy-start(f32[1,32,768]{2,1,0:T(8,128)} %param.10) | copy-start | bytes 294916
  72.4 19.3 %collective-permute-start.3 = (bf16[3,32,768]{2,1,0:T(8,128)(2,1)S(1)}, bf16[3,32,768]{2,1,0:T(8,128)(2,1)S(1)}, u32[]{:S(2)}, u32[]{:S(2)}) collective-permute-start(bf16[3,32,768]{2,1,0:T(8,128)(2,1)S(1)} %get-tuple-element.21), channel_id=1, source_target_pairs={{0,58},{2,60},{4,62},{6,0},{8,2},{10,4},{12,6},{14,8},{16,10},{18,... | collective-permute-start | bytes 442376 | tf_op jit(solution)/shard_map/ppermute | solution.py:32
  76.4 15.4 %collective-permute-start.4 = (bf16[3,32,768]{2,1,0:T(8,128)(2,1)S(1)}, bf16[3,32,768]{2,1,0:T(8,128)(2,1)S(1)}, u32[]{:S(2)}, u32[]{:S(2)}) collective-permute-start(bf16[3,32,768]{2,1,0:T(8,128)(2,1)S(1)} %get-tuple-element.22), channel_id=1, source_target_pairs={{0,6},{2,8},{4,10},{6,12},{8,14},{10,16},{12,18},{14,20},{16,22},{... | collective-permute-start | bytes 442376 | tf_op jit(solution)/shard_map/ppermute | solution.py:32
  79.6 17.8 %collective-permute-start.6 = (bf16[32,768]{1,0:T(8,128)(2,1)S(1)}, bf16[32,768]{1,0:T(8,128)(2,1)S(1)}, u32[]{:S(2)}, u32[]{:S(2)}) collective-permute-start(bf16[32,768]{1,0:T(8,128)(2,1)S(1)} %get-tuple-element.19), channel_id=1, source_target_pairs={{0,12},{2,14},{4,16},{6,18},{8,20},{10,22},{12,24},{14,26},{16,28}... | collective-permute-start | bytes 147464 | tf_op jit(solution)/shard_map/ppermute | solution.py:32
  81.5 15.9 %collective-permute-start.5 = (bf16[32,768]{1,0:T(8,128)(2,1)S(1)}, bf16[32,768]{1,0:T(8,128)(2,1)S(1)}, u32[]{:S(2)}, u32[]{:S(2)}) collective-permute-start(bf16[32,768]{1,0:T(8,128)(2,1)S(1)} %get-tuple-element.20), channel_id=1, source_target_pairs={{0,52},{2,54},{4,56},{6,58},{8,60},{10,62},{12,0},{14,2},{16,4},{1... | collective-permute-start | bytes 147464 | tf_op jit(solution)/shard_map/ppermute | solution.py:32
  97.4 15.1 %collective-permute-start.7 = (bf16[32,768]{1,0:T(8,128)(2,1)S(1)}, bf16[32,768]{1,0:T(8,128)(2,1)S(1)}, u32[]{:S(2)}, u32[]{:S(2)}) collective-permute-start(bf16[32,768]{1,0:T(8,128)(2,1)S(1)} %get-tuple-element.12), channel_id=1, source_target_pairs={{0,46},{2,48},{4,50},{6,52},{8,54},{10,56},{12,58},{14,60},{16,62}... | collective-permute-start | bytes 147464 | tf_op jit(solution)/shard_map/ppermute | solution.py:32
  109.0 15.9 %collective-permute-start.8 = (bf16[32,768]{1,0:T(8,128)(2,1)S(1)}, bf16[32,768]{1,0:T(8,128)(2,1)S(1)}, u32[]{:S(2)}, u32[]{:S(2)}) collective-permute-start(bf16[32,768]{1,0:T(8,128)(2,1)S(1)} %get-tuple-element.13), channel_id=1, source_target_pairs={{0,18},{2,20},{4,22},{6,24},{8,26},{10,28},{12,30},{14,32},{16,34}... | collective-permute-start | bytes 147464 | tf_op jit(solution)/shard_map/ppermute | solution.py:32
  125.6 16.5 %collective-permute-start.10 = (bf16[32,768]{1,0:T(8,128)(2,1)S(1)}, bf16[32,768]{1,0:T(8,128)(2,1)S(1)}, u32[]{:S(2)}, u32[]{:S(2)}) collective-permute-start(bf16[32,768]{1,0:T(8,128)(2,1)S(1)} %get-tuple-element.15), channel_id=1, source_target_pairs={{0,18},{2,20},{4,22},{6,24},{8,26},{10,28},{12,30},{14,32},{16,34}... | collective-permute-start | bytes 147464 | tf_op jit(solution)/shard_map/ppermute | solution.py:32
  128.6 15.4 %collective-permute-start.9 = (bf16[32,768]{1,0:T(8,128)(2,1)S(1)}, bf16[32,768]{1,0:T(8,128)(2,1)S(1)}, u32[]{:S(2)}, u32[]{:S(2)}) collective-permute-start(bf16[32,768]{1,0:T(8,128)(2,1)S(1)} %get-tuple-element.15), channel_id=1, source_target_pairs={{0,46},{2,48},{4,50},{6,52},{8,54},{10,56},{12,58},{14,60},{16,62}... | collective-permute-start | bytes 147464 | tf_op jit(solution)/shard_map/ppermute | solution.py:32
  142.1 28.0 %collective-permute-start.13 = (bf16[1,32,768]{2,1,0:T(8,128)(2,1)S(1)}, bf16[1,32,768]{2,1,0:T(8,128)(2,1)S(1)}, u32[]{:S(2)}, u32[]{:S(2)}) collective-permute-start(bf16[1,32,768]{2,1,0:T(8,128)(2,1)S(1)} %bitcast.66), channel_id=1, source_target_pairs={{0,12},{2,14},{4,16},{6,18},{8,20},{10,22},{12,24},{14,26},{16,28}... | collective-permute-start | bytes 147464 | tf_op jit(solution)/shard_map/ppermute | solution.py:32
  144.0 26.1 %collective-permute-start.14 = (bf16[1,32,768]{2,1,0:T(8,128)(2,1)S(1)}, bf16[1,32,768]{2,1,0:T(8,128)(2,1)S(1)}, u32[]{:S(2)}, u32[]{:S(2)}) collective-permute-start(bf16[1,32,768]{2,1,0:T(8,128)(2,1)S(1)} %bitcast.64), channel_id=1, source_target_pairs={{0,52},{2,54},{4,56},{6,58},{8,60},{10,62},{12,0},{14,2},{16,4},{1... | collective-permute-start | bytes 147464 | tf_op jit(solution)/shard_map/ppermute | solution.py:32
  154.3 15.7 %collective-permute-start.12 = (bf16[3,32,768]{2,1,0:T(8,128)(2,1)S(1)}, bf16[3,32,768]{2,1,0:T(8,128)(2,1)S(1)}, u32[]{:S(2)}, u32[]{:S(2)}) collective-permute-start(bf16[3,32,768]{2,1,0:T(8,128)(2,1)S(1)} %pad_maximum_fusion.2), channel_id=1, source_target_pairs={{0,6},{2,8},{4,10},{6,12},{8,14},{10,16},{12,18},{14,20},{16,22},{... | collective-permute-start | bytes 442376 | tf_op jit(solution)/shard_map/ppermute | solution.py:32
  156.3 13.8 %collective-permute-start.11 = (bf16[3,32,768]{2,1,0:T(8,128)(2,1)S(1)}, bf16[3,32,768]{2,1,0:T(8,128)(2,1)S(1)}, u32[]{:S(2)}, u32[]{:S(2)}) collective-permute-start(bf16[3,32,768]{2,1,0:T(8,128)(2,1)S(1)} %pad_maximum_fusion.2), channel_id=1, source_target_pairs={{0,58},{2,60},{4,62},{6,0},{8,2},{10,4},{12,6},{14,8},{16,10},{18,... | collective-permute-start | bytes 442376 | tf_op jit(solution)/shard_map/ppermute | solution.py:32
  170.2 11.8 %collective-permute-start.15 = (bf16[10,32,768]{2,1,0:T(8,128)(2,1)S(1)}, bf16[10,32,768]{2,1,0:T(8,128)(2,1)S(1)}, u32[]{:S(2)}, u32[]{:S(2)}) collective-permute-start(bf16[10,32,768]{2,1,0:T(8,128)(2,1)S(1)} %slice.60), channel_id=1, source_target_pairs={{0,62},{2,0},{4,2},{6,4},{8,6},{10,8},{12,10},{14,12},{16,14},{18,... | collective-permute-start | bytes 1474568 | tf_op jit(solution)/shard_map/ppermute | solution.py:32
  172.1 11.3 %collective-permute-start.16 = (bf16[11,32,768]{2,1,0:T(8,128)(2,1)S(1)}, bf16[11,32,768]{2,1,0:T(8,128)(2,1)S(1)}, u32[]{:S(2)}, u32[]{:S(2)}) collective-permute-start(bf16[11,32,768]{2,1,0:T(8,128)(2,1)S(1)} %constant_dynamic-update-slice_fusion), channel_id=1, source_target_pairs={{0,2},{2,4},{4,6},{6,8},{8,10},{10,12},{12,14},{14,16},{16,18},{18... | collective-permute-start | bytes 1622024 | tf_op jit(solution)/shard_map/ppermute | solution.py:32
  184.3 15.6 %copy-start.1 = (bf16[768,768]{1,0:T(8,128)(2,1)}, bf16[768,768]{1,0:T(8,128)(2,1)S(1)}, u32[]{:S(2)}) copy-start(bf16[768,768]{1,0:T(8,128)(2,1)S(1)} %fusion.own_ref) | copy-start | bytes 3538948
  184.3 15.6 %collective-permute-start.17 = (bf16[768,768]{1,0:T(8,128)(2,1)S(1)}, bf16[768,768]{1,0:T(8,128)(2,1)S(1)}, u32[]{:S(2)}, u32[]{:S(2)}) collective-permute-start(bf16[768,768]{1,0:T(8,128)(2,1)S(1)} %fusion.own_ref), channel_id=1, source_target_pairs={{0,1},{1,0},{2,3},{3,2},{4,5},{5,4},{6,7},{7,6},{8,9},{9,8},{10,11... | collective-permute-start | bytes 3538952 | tf_op jit(solution)/shard_map/ppermute | solution.py:36
  199.9 1.0 copy-start.2
